TPU v7x, 128 devices: a whole 4x4x4 slice. The times are simulated.
128 devices in a mesh: chan: 8 (over y_lo, z), freq: 16 (over y_hi, x, core).
Axes of the slice: x: 4, y: 4 (y_hi: 2, y_lo: 2; y = y_hi * 2 + y_lo), z: 4, core: 2. Of those that a mesh axis runs over, the one named last changes fastest.
Arguments:
- spectra: bfloat16 [2, 32, 256, 1024], P(None, None, 'freq', 'chan'), may hold values from -6 to 6
- block_position: int32 [8], replicated, may hold values from 0 to 7, each once
Outputs:
- taup: float32 [8, 256, 512], P('chan', 'freq')
Inputs may be any that keep to these rules, and one draw needn't show every extreme that they name: block_position is a permutation: every fiber position 0 to 7 holds exactly one stored block; group k of the chan axis stores block k.
All inputs are finite; a program needn't handle non-finite values.
Results may differ from a plain program's by a relative error of at most 0.0003.
Values may be sent and summed in bfloat16 or wider, within the bound.
A program may use at most 64 MiB of HBM per device.

v0:
```python
import math

import jax
import jax.numpy as jnp
from jax import lax
from jax.sharding import PartitionSpec as P

SEGMENTS = 32
FREQS = 256
BLOCK = 128
SLOWNESS = 256
LAG_TIMES = 512


def passed_along(value, axis, steps):
    count = lax.axis_size(axis)
    pairs = [(source, (source + steps) % count) for source in range(count)]
    return lax.ppermute(value, axis, pairs)


def lag_sums(panel):
    leading = panel.shape[:-2]
    extent = panel.shape[-1]
    flat_panel = panel.reshape(leading + (extent * extent,))
    padded = jnp.pad(flat_panel, [(0, 0)] * len(leading) + [(0, extent)])
    skewed = padded.reshape(leading + (extent, extent + 1))
    row_index = lax.broadcasted_iota(jnp.int32, (extent, extent + 1), 0)
    col_index = lax.broadcasted_iota(jnp.int32, (extent, extent + 1), 1)
    before_wrap = row_index + col_index < extent
    forward_lags = jnp.sum(jnp.where(before_wrap, skewed, 0.0), axis=-2)
    backward_lags = jnp.sum(skewed, axis=-2) - forward_lags
    return jnp.concatenate([backward_lags[..., 1:], forward_lags[..., :extent]], axis=-1)


def angles(numerator):
    modulus = 8 * FREQS * BLOCK
    return jnp.mod(numerator, modulus).astype(jnp.float32) * (2.0 * math.pi / modulus)


def inverse_counts(delta_count, nblocks):
    deltas = lax.broadcasted_iota(jnp.int32, (delta_count, 2 * BLOCK), 0)
    lag_value = lax.broadcasted_iota(jnp.int32, (delta_count, 2 * BLOCK), 1) - BLOCK
    counts = SEGMENTS * (nblocks - deltas) * (BLOCK - jnp.abs(lag_value))
    usable = (lag_value > -BLOCK) & ((deltas >= 1) | (lag_value >= 1))
    inverse = jnp.where(usable, 1.0 / jnp.maximum(counts, 1).astype(jnp.float32), 0.0)
    return jnp.concatenate([inverse, inverse], axis=-1)


def slant_terms(means_block, freq_ids, delta_start, group_blocks):
    bins, delta_count = (means_block.shape[0], means_block.shape[1])
    slow_index = lax.broadcasted_iota(jnp.int32, (1, 1, SLOWNESS), 2) - SLOWNESS // 2
    lag_value = lax.broadcasted_iota(jnp.int32, (1, 2 * BLOCK, 1), 1) - BLOCK
    freq_column = freq_ids.reshape(bins, 1, 1)
    lag_angle = angles(freq_column * slow_index * lag_value)
    cosine = jnp.cos(lag_angle)
    sine_part = jnp.sin(lag_angle)
    lag_table = jnp.concatenate(
        [jnp.concatenate([cosine, sine_part], -1), jnp.concatenate([-sine_part, cosine], -1)], 1
    )
    rotated = jnp.einsum("fdk,fkp->fdp", means_block, lag_table, precision=lax.Precision.HIGHEST)
    deltas = delta_start + lax.broadcasted_iota(jnp.int32, (1, delta_count, 1), 1)
    offset_angle = angles(freq_column * slow_index * (BLOCK * deltas))
    offset_cos = jnp.cos(offset_angle)
    offset_sin = jnp.sin(offset_angle)
    real_part = rotated[..., :SLOWNESS]
    imag_part = rotated[..., SLOWNESS:]
    shifted_re = real_part * offset_cos - imag_part * offset_sin
    shifted_im = real_part * offset_sin + imag_part * offset_cos
    apertures = delta_count // group_blocks
    summed_re = shifted_re.reshape(bins, apertures, group_blocks, SLOWNESS).sum(axis=2)
    summed_im = shifted_im.reshape(bins, apertures, group_blocks, SLOWNESS).sum(axis=2)
    lag_time = lax.broadcasted_iota(jnp.int32, (1, LAG_TIMES), 1) - LAG_TIMES // 2
    time_angle = angles(freq_ids.reshape(bins, 1) * (4 * BLOCK * lag_time))
    spectrum = jnp.concatenate([summed_re, summed_im], axis=0)
    kernel = jnp.concatenate([jnp.cos(time_angle), -jnp.sin(time_angle)], axis=0)
    result = jnp.einsum("gas,gt->ast", spectrum, kernel, precision=lax.Precision.HIGHEST)
    return result.reshape(apertures * SLOWNESS, LAG_TIMES)


def slant_all(mean_stacks, freq_start, delta_start, group_blocks):
    freq_count, delta_count = (mean_stacks.shape[0], mean_stacks.shape[1])
    block_bins = 4
    block_total = freq_count // block_bins
    blocks = mean_stacks.reshape(block_total, block_bins, delta_count, 4 * BLOCK)
    freq_table = (freq_start + jnp.arange(freq_count, dtype=jnp.int32)).reshape(
        block_total, block_bins
    )

    def add_block(running, block_item):
        return (
            running + slant_terms(block_item[0], block_item[1], delta_start, group_blocks),
            None,
        )

    initial = jnp.zeros((delta_count // group_blocks * SLOWNESS, LAG_TIMES), jnp.float32)
    summed, unused = lax.scan(add_block, initial, (blocks, freq_table))
    return summed


def cross_stack(first_spec, second_spec, first_pos, second_pos, drop_backward, nblocks):
    window_rows = 2 * first_spec.shape[1]
    freq_dev = first_spec.shape[2]
    first_width, second_width = (first_spec.shape[3], second_spec.shape[3])
    first_count, second_count = (first_width // BLOCK, second_width // BLOCK)
    block_bins = 2
    block_total = freq_dev // block_bins
    left_side = jnp.concatenate([first_spec[0], first_spec[1]], axis=0)
    right_side = jnp.stack(
        [
            jnp.concatenate([second_spec[0], second_spec[1]], axis=0),
            jnp.concatenate([second_spec[1], -second_spec[0]], axis=0),
        ],
        axis=2,
    )
    left_blocks = jnp.moveaxis(
        left_side.reshape(window_rows, block_total, block_bins, first_count, BLOCK), 1, 0
    )
    right_blocks = jnp.moveaxis(
        right_side.reshape(window_rows, block_total, block_bins, 2, second_count, BLOCK), 1, 0
    )
    block_delta = second_pos[None, :] - first_pos[:, None]
    forward = (block_delta >= 0)[None, :, :, None]
    if drop_backward:
        panel_weight = (block_delta >= 0).astype(jnp.float32)
    else:
        panel_weight = jnp.ones(block_delta.shape, jnp.float32)
    targets = lax.broadcasted_iota(jnp.int32, (nblocks, 1), 0)
    selector = (jnp.abs(block_delta) == targets).astype(jnp.float32) * panel_weight

    def one_block(block_item):
        panels = jnp.einsum(
            "kfar,kfpbe->fabpre", block_item[0], block_item[1], preferred_element_type=jnp.float32
        )
        lag_block = lag_sums(panels)
        real_lags = lag_block[..., 0, :]
        imag_lags = lag_block[..., 1, :]
        flipped_re = jnp.roll(jnp.flip(real_lags, -1), 1, -1)
        flipped_im = jnp.roll(jnp.flip(imag_lags, -1), 1, -1)
        oriented = jnp.concatenate(
            [jnp.where(forward, real_lags, flipped_re), jnp.where(forward, imag_lags, -flipped_im)],
            axis=-1,
        )
        oriented = oriented.reshape(block_bins, first_count * second_count, 4 * BLOCK)
        return jnp.einsum("dp,fpk->fdk", selector, oriented, precision=lax.Precision.HIGHEST)

    block_parts = lax.map(one_block, (left_blocks, right_blocks))
    return block_parts.reshape(freq_dev, nblocks, 4 * BLOCK)


def shards(spectra, block_position):
    groups = lax.axis_size("chan")
    own_group = lax.axis_index("chan")
    freq_dev = spectra.shape[2]
    group_blocks = spectra.shape[3] // BLOCK
    nblocks = groups * group_blocks
    freq_start = lax.axis_index("freq") * freq_dev
    half_loop = groups // 2

    def positions(group_index):
        return lax.dynamic_slice_in_dim(
            block_position, jnp.mod(group_index, groups) * group_blocks, group_blocks
        )

    own_pos = positions(own_group)
    stacks = cross_stack(spectra, spectra, own_pos, own_pos, True, nblocks)
    moving = spectra
    for distance in range(1, half_loop + 1):
        moving = passed_along(moving, "chan", 1)
        if distance < half_loop:
            stacks = stacks + cross_stack(
                spectra, moving, own_pos, positions(own_group - distance), False, nblocks
            )
        else:
            second_spec = moving
            second_group = own_group - distance
            keeps_pair = jnp.mod(own_group, groups) < jnp.mod(second_group, groups)
            first_pos = positions(own_group)
            second_pos = positions(second_group)
            stacks = stacks + lax.cond(
                keeps_pair,
                lambda: cross_stack(spectra, second_spec, first_pos, second_pos, False, nblocks),
                lambda: jnp.zeros((freq_dev, nblocks, 4 * BLOCK), jnp.float32),
            )
    out_scale = math.sqrt(SEGMENTS / (FREQS * group_blocks))
    mean_stacks = stacks * inverse_counts(nblocks, nblocks)[None]
    image_term = slant_all(mean_stacks, freq_start, 0, group_blocks)
    summed_image = lax.psum_scatter(image_term, ("chan", "freq"), scatter_dimension=0, tiled=True)
    return (summed_image * out_scale).reshape(1, summed_image.shape[0], summed_image.shape[1])


def solution(mesh):
    return jax.shard_map(
        shards,
        mesh=mesh,
        in_specs=(P(None, None, "freq", "chan"), P()),
        out_specs=P("chan", "freq", None),
        check_vma=False,
    )
```

profile of v0, /device:TPU:1, one launch (start us, length us, event | category | flops | bytes accessed | tf_op | source)
XLA Modules:
  0.0 868.5 jit_solution(1690590579600440833)
XLA Ops:
  6.5 1.0 copy.37
  7.6 2.5 collective-permute-start
  10.1 1.0 fusion.95
  11.4 21.4 %while.79 = (s32[]{:T(128)}, f32[8,2,8,512]{3,2,1,0:T(8,128)S(1)}, bf16[8,64,2,2,1,128]{5,1,3,2,4,0:T(8,128)(2,1)S(1)}, bf16[8,64,2,1,128]{4,1,2,3,0:T(8,128)(2,1)S(1)}, s32[]{:T(128)}, /*index=5*/f32[]{:T(128)}) while((s32[]{:T(128)}, f32[8,2,8,512]{3,2,1,0:T(8,128)S(1)}, bf16[8,64,2,2,1,128]{5,1,3,2,4,0:T(8,128)(2,1)S(1)}, ...), condition=%wide.region_3.4_spmd.clone, body=%wide.region_0.3_spmd.clone.sunk | while | flops 8629514 | bytes 3106709 | solution.py:146
  11.8 0.8 pad_reduce_fusion.10
  14.5 0.8 pad_reduce_fusion.10
  17.2 0.8 pad_reduce_fusion.10
  19.8 0.8 pad_reduce_fusion.10
  22.5 0.8 pad_reduce_fusion.10
  25.2 0.8 pad_reduce_fusion.10
  27.9 0.8 pad_reduce_fusion.10
  30.5 0.8 pad_reduce_fusion.10
  37.4 1.7 collective-permute-start.1
  39.1 27.6 %while.80 = (s32[]{:T(128)}, f32[8,2,8,512]{3,2,1,0:T(8,128)S(1)}, pred[1,1,1,1]{3,2,1,0:T(4,128)(4,1)}, bf16[8,64,2,2,1,128]{5,1,3,2,4,0:T(8,128)(2,1)S(1)}, bf...) while((s32[]{:T(128)}, f32[8,2,8,512]{3,2,1,0:T(8,128)S(1)}, ...), condition=%wide.region_7.8_spmd.clone, body=%wide.region_4.7_spmd.clone.sunk | while | flops 8632074 | bytes 3143562 | solution.py:146
  39.5 0.8 pad_reduce_fusion.11
  43.0 0.8 pad_reduce_fusion.11
  46.4 0.8 pad_reduce_fusion.11
  49.9 0.8 pad_reduce_fusion.11
  53.3 0.8 pad_reduce_fusion.11
  56.8 0.8 pad_reduce_fusion.11
  60.2 0.8 pad_reduce_fusion.11
  63.7 0.8 pad_reduce_fusion.11
  66.8 1.4 collective-permute-start.2
  68.3 27.6 %while.81 = (s32[]{:T(128)}, f32[8,2,8,512]{3,2,1,0:T(8,128)S(1)}, pred[1,1,1,1]{3,2,1,0:T(4,128)(4,1)}, bf16[8,64,2,2,1,128]{5,1,3,2,4,0:T(8,128)(2,1)S(1)}, bf...) while((s32[]{:T(128)}, f32[8,2,8,512]{3,2,1,0:T(8,128)S(1)}, ...), condition=%wide.region_11.12_spmd.clone, body=%wide.region_8.11_spmd.clone.sunk | while | flops 8632074 | bytes 3143562 | solution.py:146
  68.7 0.8 pad_reduce_fusion.12
  72.2 0.8 pad_reduce_fusion.12
  75.6 0.8 pad_reduce_fusion.12
  79.1 0.8 pad_reduce_fusion.12
  82.5 0.8 pad_reduce_fusion.12
  86.0 0.8 pad_reduce_fusion.12
  89.4 0.8 pad_reduce_fusion.12
  92.9 0.8 pad_reduce_fusion.12
  96.4 27.6 %while.82 = (s32[]{:T(128)}, f32[8,2,8,512]{3,2,1,0:T(8,128)S(1)}, pred[1,1,1,1]{3,2,1,0:T(4,128)(4,1)}, bf16[8,64,2,2,1,128]{5,1,3,2,4,0:T(8,128)(2,1)S(1)}, bf...) while((s32[]{:T(128)}, f32[8,2,8,512]{3,2,1,0:T(8,128)S(1)}, ...), condition=%wide.region_15.16_spmd.clone, body=%wide.region_12.15_spmd.clone.sunk | while | flops 8632074 | bytes 3143562 | solution.py:146
  96.8 0.8 pad_reduce_fusion.13
  100.3 0.8 pad_reduce_fusion.13
  103.7 0.8 pad_reduce_fusion.13
  107.2 0.8 pad_reduce_fusion.13
  110.6 0.8 pad_reduce_fusion.13
  124.1 34.6 %conditional.1 = (f32[16,8,512]{2,1,0:T(8,128)}) conditional(s32[]{:T(128)} %convert_element_type.94, () %tuple.90, (bf16[2,32,16,128]{3,2,1,0:T(8,128)(2,1)S(1)}, bf16[2,32,16,128]{3,1,2,0:T(8,128)(2,1)S(1)}, s32[8]{0:T(128)S(1)}, s32[1]{0:T(128)}, s32[]{:T(128)}, /*index=5*/s32[]{:T(128)}, s32[]{:T(128)}, s32[]{:T(128)}, s32[]{:T(128)}) %tuple.252), branch_computations={%region_16.17_spmd, %region_17.22_spmd} | conditional | flops 11319056 | bytes 6420037 | solution.py:179
  126.2 32.5 %while.78 = (s32[]{:T(128)}, f32[8,2,8,512]{3,2,1,0:T(8,128)}, pred[1,1,1,1]{3,2,1,0:T(4,128)(4,1)}, bf16[8,64,2,2,1,128]{5,1,3,2,4,0:T(8,128)(2,1)S(1)}, bf16[8...) while((s32[]{:T(128)}, f32[8,2,8,512]{3,2,1,0:T(8,128)}, ...), condition=%wide.region_21.21_spmd.clone, body=%wide.region_18.20_spmd.clone.sunk | while | flops 8632074 | bytes 3143082 | solution.py:146
  158.7 1.0 fusion.87
  159.7 53.2 %while.83 = (s32[]{:T(128)}, f32[2048,512]{1,0:T(8,128)}, f32[4,4,8,512]{3,2,1,0:T(8,128)S(1)}, s32[4,4]{1,0:T(4,128)S(1)}, s32[]{:T(128)}, /*index=5*/s32[]{:T(128)}) while((s32[]{:T(128)}, f32[2048,512]{1,0:T(8,128)}, f32[4,4,8,512]{3,2,1,0:T(8,128)S(1)}, s32[4,4]{1,0:T(4,128)S(1)}, s32[]{:T(128)}, ...), condition=%wide.region_23.24_spmd.clone, body=%wide.region_22.23_spmd.clone.sunk | while | flops 210718976 | bytes 57134356 | solution.py:96
  160.0 4.2 fusion.144
  164.2 2.1 fusion.145
  166.5 3.5 fusion.147
  170.0 1.1 bitcast_add_fusion.3
  171.1 1.9 copy-done.1
  173.3 4.2 fusion.144
  177.4 2.1 fusion.145
  179.8 3.5 fusion.147
  183.3 1.1 bitcast_add_fusion.3
  184.4 1.9 copy-done.1
  186.5 4.2 fusion.144
  190.7 2.1 fusion.145
  193.1 3.5 fusion.147
  196.5 1.1 bitcast_add_fusion.3
  197.7 1.9 copy-done.1
  199.8 4.2 fusion.144
  204.0 2.1 fusion.145
  206.3 3.5 fusion.147
  209.8 1.1 bitcast_add_fusion.3
  210.9 1.9 copy-done.1
  212.9 647.4 %reduce-scatter.2.cloned.1.call-done = f32[16,512]{1,0:T(8,128)} async-done(((f32[2048,512]{1,0:T(8,128)}), f32[16,512]{1,0:T(8,128)}) %reduce-scatter.2.cloned.1.call-update) | async-done | bytes 32784 | tf_op jit(solution)/shard_map/reduce_scatter | solution.py:187
  860.3 1.4 multiply_bitcast_fusion
  (910 shorter events, 115.6 us)
Async XLA Ops:
  6.5 853.7 %reduce-scatter.2.cloned.1.call-start = ((), (), s32[]{:S(2)}) async-start(), calls=%async_computation.1 | async-start | bytes 4227072 | tf_op jit(solution)/shard_map/reduce_scatter | solution.py:187
  7.6 29.7 %collective-permute-start = (bf16[2,32,16,128]{3,1,2,0:T(8,128)(2,1)S(1)}, bf16[2,32,16,128]{3,1,2,0:T(8,128)(2,1)S(1)}, u32[]{:S(2)}, u32[]{:S(2)}) collective-permute-start(bf16[2,32,16,128]{3,1,2,0:T(8,128)(2,1)S(1)} %copy.37), channel_id=1, source_target_pairs={{0,16},{16,32},{32,48},{48,64},{64,80},{80,96},{96,112},{112,0},{1... | collective-permute-start | bytes 786440 | tf_op jit(solution)/shard_map/ppermute | solution.py:18
  11.4 21.6 %copy-start.3 = (s32[8]{0:T(128)S(1)}, s32[8]{0:T(128)}, u32[]{:S(2)}) copy-start(s32[8]{0:T(128)} %param.17) | copy-start | bytes 100
  37.4 29.3 %collective-permute-start.1 = (bf16[2,32,16,128]{3,1,2,0:T(8,128)(2,1)S(1)}, bf16[2,32,16,128]{3,1,2,0:T(8,128)(2,1)S(1)}, u32[]{:S(2)}, u32[]{:S(2)}) collective-permute-start(bf16[2,32,16,128]{3,1,2,0:T(8,128)(2,1)S(1)} %collective-permute-done), channel_id=1, source_target_pairs={{0,16},{16,32},{32,48},{48,64},{64,80},{80,96},{96,112},{112,0},{1... | collective-permute-start | bytes 786440 | tf_op jit(solution)/shard_map/ppermute | solution.py:18
  66.8 29.1 %collective-permute-start.2 = (bf16[2,32,16,128]{3,1,2,0:T(8,128)(2,1)S(1)}, bf16[2,32,16,128]{3,1,2,0:T(8,128)(2,1)S(1)}, u32[]{:S(2)}, u32[]{:S(2)}) collective-permute-start(bf16[2,32,16,128]{3,1,2,0:T(8,128)(2,1)S(1)} %collective-permute-done.1), channel_id=1, source_target_pairs={{0,16},{16,32},{32,48},{48,64},{64,80},{80,96},{96,112},{112,0},{1... | collective-permute-start | bytes 786440 | tf_op jit(solution)/shard_map/ppermute | solution.py:18
  96.0 28.1 %collective-permute-start.3 = (bf16[2,32,16,128]{3,1,2,0:T(8,128)(2,1)S(1)}, bf16[2,32,16,128]{3,1,2,0:T(8,128)(2,1)S(1)}, u32[]{:S(2)}, u32[]{:S(2)}) collective-permute-start(bf16[2,32,16,128]{3,1,2,0:T(8,128)(2,1)S(1)} %collective-permute-done.2), channel_id=1, source_target_pairs={{0,16},{16,32},{32,48},{48,64},{64,80},{80,96},{96,112},{112,0},{1... | collective-permute-start | bytes 786440 | tf_op jit(solution)/shard_map/ppermute | solution.py:18
  96.4 27.8 %copy-start.2 = (bf16[2,32,16,128]{3,2,1,0:T(8,128)(2,1)S(1)}, bf16[2,32,16,128]{3,2,1,0:T(8,128)(2,1)}, u32[]{:S(2)}) copy-start(bf16[2,32,16,128]{3,2,1,0:T(8,128)(2,1)} %param.16) | copy-start | bytes 786436
  164.1 5.8 copy-start
  171.1 1.9 copy-start.1
  177.4 5.8 copy-start
  184.4 1.9 copy-start.1
  190.7 5.8 copy-start
  197.6 1.9 copy-start.1
  204.0 5.8 copy-start
  210.9 1.9 copy-start.1
Sparse Core Ops, SparseCore 0:
  213.0 647.2 reduce-scatter.1
where the time goes:
time: 875 us; the launch traced here: 868 us
  waiting for transfers between devices  647 us (74%)
  local copies, waits for them, and re-layouts  115 us (13%)
  other arithmetic  46 us (5%)
  matrix products  31.8 us (4%)
  between operations  17.2 us (2%)
    reduce_scatter x1, waiting for transfers between devices, shards(): lax.psum_scatter(image_term, ('chan', 'freq'), scatter_dimension=0, tiled...  647 us
    reshape x80, local copies, waits for them, and re-layouts, lag_sums(): skewed = padded.reshape(leading + (extent, extent + 1))  46.4 us
    pad x40, local copies, waits for them, and re-layouts, lag_sums(): padded = jnp.pad(flat_panel, [(0, 0)] * len(leading) + [(0, extent)])  31.1 us
    while x184, local copies, waits for them, and re-layouts  24.3 us
  transfers between devices with their start and end apart: 5, of which 1 were waited for; matrix products, arithmetic and copies ran while one was open for 12% of the time, Pallas kernels for 0%

commit v1 on v0

v1 whole, which is shorter than its diff:
```python
import functools
import math

import jax
import jax.numpy as jnp
from jax import lax
from jax.experimental import pallas as pl
from jax.experimental.pallas import tpu as pltpu
from jax.sharding import PartitionSpec as P

SEGMENTS = 32
FREQS = 256
BLOCK = 128
SLOWNESS = 256
LAG_TIMES = 512
CHAN = 8
FREQ = 16
BINS = 2
ROWS = 2 * SEGMENTS * BINS
TURN = 8 * FREQS * BLOCK
WIDE = 32
SLABS = SLOWNESS // WIDE
SINE = [(-1) ** k * (2 * math.pi) ** (2 * k + 1) / math.factorial(2 * k + 1) for k in range(7)]


def iota(shape, axis):
    return lax.broadcasted_iota(jnp.int32, shape, axis)


def cosine(steps):
    centered = (steps & (TURN - 1)) - TURN // 2
    turn = jnp.abs(centered).astype(jnp.float32) * (1.0 / TURN) - 0.25
    square = turn * turn
    value = SINE[-1]
    for coefficient in SINE[-2::-1]:
        value = value * square + coefficient
    return value * turn


QUARTER = TURN // 4


def lag_at(place):
    return jnp.where(place < BLOCK, place + 1, place - 2 * BLOCK + 1)


def split(value):
    high = value.astype(jnp.bfloat16)
    low = (value - high.astype(jnp.float32)).astype(jnp.bfloat16)
    return high, low


def dot(left, right):
    return jnp.dot(left, right, preferred_element_type=jnp.float32)


def kernel(
    position_ref,
    spectra_ref,
    out_ref,
    blocks,
    left,
    right,
    weight_cos,
    weight_sin,
    lag_high,
    lag_low,
    time_high,
    time_low,
    terms,
    gathered,
    relayed,
    received,
    turned,
    flipped,
    own_sem,
    send_first,
    recv_first,
    send_second,
    recv_second,
    send_third,
    recv_third,
):
    chan = lax.axis_index("chan")
    freq = lax.axis_index("freq")

    barrier = pltpu.get_barrier_semaphore()
    for step in range(1, CHAN):
        pl.semaphore_signal(
            barrier,
            inc=1,
            device_id={"chan": lax.rem(chan + step, CHAN)},
            device_id_type=pl.DeviceIdType.MESH,
        )
    for step in range(1, FREQ):
        pl.semaphore_signal(
            barrier,
            inc=1,
            device_id={"freq": lax.rem(freq + step, FREQ)},
            device_id_type=pl.DeviceIdType.MESH,
        )
    own = pltpu.make_async_copy(spectra_ref.at[:, chan], blocks.at[chan], own_sem)
    own.start()
    pl.semaphore_wait(barrier, CHAN - 1 + FREQ - 1)

    first = []
    for step in range(1, CHAN):
        peer = lax.rem(chan + step, CHAN)
        copy = pltpu.make_async_remote_copy(
            src_ref=spectra_ref.at[:, peer],
            dst_ref=blocks.at[chan],
            send_sem=send_first.at[step],
            recv_sem=recv_first.at[step],
            device_id={"chan": peer},
            device_id_type=pl.DeviceIdType.MESH,
        )
        copy.start()
        first.append(copy)

    base_bin = 2 * CHAN * freq + 2 * chan

    row = iota((CHAN * SLABS, 2 * BLOCK), 0)
    lane = iota((CHAN * SLABS, 2 * BLOCK), 1)
    offset_bin = row // SLABS
    slow = WIDE * (row % SLABS) - SLOWNESS // 2
    lag = lag_at(lane)
    count = SEGMENTS * (CHAN - offset_bin) * (BLOCK - jnp.abs(lag))
    usable = (jnp.abs(lag) < BLOCK) & ((offset_bin >= 1) | (lag >= 1))
    inverse = jnp.where(usable, 1.0 / jnp.maximum(count, 1).astype(jnp.float32), 0.0)
    for bin_index in range(BINS):
        steps = (base_bin + bin_index) * slow * (BLOCK * offset_bin + lag)
        weight_cos[bin_index] = cosine(steps) * inverse
        weight_sin[bin_index] = cosine(steps - QUARTER) * inverse

    for bin_index in range(BINS):
        row = iota((2 * BLOCK, 2 * BLOCK), 0)
        lane = iota((2 * BLOCK, 2 * BLOCK), 1)
        lag = lag_at(row)
        slow = lane % WIDE
        part = (lane // WIDE) % 2
        lane_bin = (lane // (2 * WIDE)) % BINS
        swapped = lane // (2 * BINS * WIDE)
        steps = (base_bin + bin_index) * slow * lag
        quarter = jnp.where(swapped == 0, -part, 1 - part)
        for row_part in range(2):
            turned_steps = steps + QUARTER * (quarter + row_part)
            table = jnp.where(lane_bin == bin_index, cosine(turned_steps), 0.0)
            high, low = split(table)
            at = pl.ds((2 * bin_index + row_part) * 2 * BLOCK, 2 * BLOCK)
            lag_high[at, :] = high
            lag_low[at, :] = low

    scale = math.sqrt(SEGMENTS / FREQS)
    for bin_index in range(BINS):
        for part in range(2):
            row = iota((CHAN * FREQ, LAG_TIMES), 0)
            time = iota((CHAN * FREQ, LAG_TIMES), 1) - LAG_TIMES // 2
            steps = (2 * row + bin_index) * time * (4 * BLOCK)
            high, low = split(cosine(steps + QUARTER * part) * scale)
            at = pl.ds((2 * bin_index + part) * CHAN * FREQ, CHAN * FREQ)
            time_high[at, :] = high
            time_low[at, :] = low

    own.wait()
    for copy in first:
        copy.wait_recv()

    odd = iota((BLOCK, ROWS), 1) % 2
    mirror = iota((BLOCK, BLOCK), 0) + iota((BLOCK, BLOCK), 1) == BLOCK - 1
    mirror = jnp.where(mirror, 1.0, 0.0).astype(jnp.bfloat16)
    for place in range(CHAN):
        block = jnp.int32(0)
        for index in range(CHAN):
            block = jnp.where(position_ref[index] == place, index, block)
        value = blocks[block].reshape(ROWS, BLOCK)
        half = ROWS // 2
        right[pl.ds(place * ROWS, ROWS), pl.ds(0, BLOCK)] = value
        right[pl.ds(place * ROWS, half), pl.ds(BLOCK, BLOCK)] = value[half:]
        right[pl.ds(place * ROWS + half, half), pl.ds(BLOCK, BLOCK)] = -value[:half]
        across = lax.dot_general(
            mirror, value, (((1,), (1,)), ((), ())), preferred_element_type=jnp.float32
        )
        for bin_index in range(BINS):
            left[pl.ds(bin_index * BLOCK, BLOCK), pl.ds(place * ROWS, ROWS)] = jnp.where(
                odd == bin_index, across, 0.0
            ).astype(jnp.bfloat16)

    wrapped = iota((BLOCK, BLOCK), 0) > iota((BLOCK, BLOCK), 1)
    for delta in range(CHAN):
        depth = (CHAN - delta) * ROWS
        panels = dot(left[:, :depth], right[delta * ROWS :, :])
        sums = []
        for bin_index in range(BINS):
            for part in range(2):
                panel = panels[
                    bin_index * BLOCK : (bin_index + 1) * BLOCK, part * BLOCK : (part + 1) * BLOCK
                ]
                skewed = pltpu.roll(panel, 0, 1, stride=1, stride_axis=0)
                ahead = jnp.sum(jnp.where(wrapped, skewed, 0.0), axis=0, keepdims=True)
                behind = jnp.sum(jnp.where(wrapped, 0.0, skewed), axis=0, keepdims=True)
                sums.append(jnp.concatenate([ahead, behind], axis=1))
        at = pl.ds(delta * SLABS, SLABS)
        pieces = []
        for bin_index in range(BINS):
            real, imag = sums[2 * bin_index], sums[2 * bin_index + 1]
            by_cos = weight_cos[bin_index, at, :]
            by_sin = weight_sin[bin_index, at, :]
            pieces.append(real * by_cos - imag * by_sin)
            pieces.append(real * by_sin + imag * by_cos)
        turned[at, :] = jnp.concatenate(pieces, axis=1)

    high, low = split(turned[...])
    slants = dot(high, lag_high[...]) + dot(low, lag_high[...]) + dot(high, lag_low[...])
    row = iota((CHAN * SLABS, BLOCK), 0)
    lane = iota((CHAN * SLABS, BLOCK), 1)
    steps = (base_bin + lane // (2 * WIDE)) * (lane % WIDE) * (BLOCK * (row // SLABS))
    terms[...] = slants[:, :BLOCK] * cosine(steps) + slants[:, BLOCK:] * cosine(steps - QUARTER)

    second = []
    for step in range(1, CHAN):
        peer = lax.rem(chan + step, CHAN)
        copy = pltpu.make_async_remote_copy(
            src_ref=terms.at[pl.ds(pl.multiple_of(peer * SLABS, SLABS), SLABS), :],
            dst_ref=gathered.at[chan],
            send_sem=send_second.at[step],
            recv_sem=recv_second.at[step],
            device_id={"chan": peer},
            device_id_type=pl.DeviceIdType.MESH,
        )
        copy.start()
        second.append(copy)
    gathered[chan] = terms[pl.ds(pl.multiple_of(chan * SLABS, SLABS), SLABS), :]
    for copy in second:
        copy.wait_recv()

    for slab in range(SLABS):
        relayed[slab] = gathered[:, slab, :]

    third = []
    for step in range(1, FREQ):
        peer = lax.rem(freq + step, FREQ)
        copy = pltpu.make_async_remote_copy(
            src_ref=relayed.at[peer // 2],
            dst_ref=received.at[freq],
            send_sem=send_third.at[step],
            recv_sem=recv_third.at[step],
            device_id={"freq": peer},
            device_id_type=pl.DeviceIdType.MESH,
        )
        copy.start()
        third.append(copy)
    received[freq] = relayed[freq // 2]
    for copy in third:
        copy.wait_recv()

    flipped[...] = received[...].reshape(FREQ * CHAN, BLOCK).T
    half_wide = WIDE // 2
    start = pl.multiple_of(lax.rem(freq, 2) * half_wide, half_wide)
    spectrum = jnp.concatenate(
        [flipped[pl.ds(start + WIDE * index, half_wide), :] for index in range(2 * BINS)],
        axis=1,
    )
    high, low = split(spectrum)
    out_ref[...] = dot(high, time_high[...]) + dot(low, time_high[...]) + dot(high, time_low[...])

    for copy in first + second + third:
        copy.wait_send()


def shards(spectra, block_position):
    pairs = spectra.shape[2] // BINS
    view = spectra.reshape(2 * SEGMENTS, pairs, BINS, BLOCK)
    image = pl.pallas_call(
        kernel,
        out_shape=jax.ShapeDtypeStruct((SLOWNESS // FREQ, LAG_TIMES), jnp.float32),
        in_specs=[
            pl.BlockSpec(memory_space=pltpu.SMEM),
            pl.BlockSpec(memory_space=pl.ANY),
        ],
        out_specs=pl.BlockSpec(memory_space=pltpu.VMEM),
        scratch_shapes=[
            pltpu.VMEM((CHAN, 2 * SEGMENTS, BINS, BLOCK), jnp.bfloat16),
            pltpu.VMEM((BINS * BLOCK, CHAN * ROWS), jnp.bfloat16),
            pltpu.VMEM((CHAN * ROWS, 2 * BLOCK), jnp.bfloat16),
            pltpu.VMEM((BINS, CHAN * SLABS, 2 * BLOCK), jnp.float32),
            pltpu.VMEM((BINS, CHAN * SLABS, 2 * BLOCK), jnp.float32),
            pltpu.VMEM((BINS * 4 * BLOCK, 2 * BLOCK), jnp.bfloat16),
            pltpu.VMEM((BINS * 4 * BLOCK, 2 * BLOCK), jnp.bfloat16),
            pltpu.VMEM((2 * FREQS, LAG_TIMES), jnp.bfloat16),
            pltpu.VMEM((2 * FREQS, LAG_TIMES), jnp.bfloat16),
            pltpu.VMEM((CHAN * SLABS, BLOCK), jnp.float32),
            pltpu.VMEM((CHAN, SLABS, BLOCK), jnp.float32),
            pltpu.VMEM((SLABS, CHAN, BLOCK), jnp.float32),
            pltpu.VMEM((FREQ, CHAN, BLOCK), jnp.float32),
            pltpu.VMEM((CHAN * SLABS, BINS * 4 * BLOCK), jnp.float32),
            pltpu.VMEM((BLOCK, FREQ * CHAN), jnp.float32),
            pltpu.SemaphoreType.DMA,
            pltpu.SemaphoreType.DMA((CHAN,)),
            pltpu.SemaphoreType.DMA((CHAN,)),
            pltpu.SemaphoreType.DMA((CHAN,)),
            pltpu.SemaphoreType.DMA((CHAN,)),
            pltpu.SemaphoreType.DMA((FREQ,)),
            pltpu.SemaphoreType.DMA((FREQ,)),
        ],
        compiler_params=pltpu.CompilerParams(collective_id=0, has_side_effects=True),
        name="slant_stack",
    )(block_position, view)
    return image.reshape(1, image.shape[0], image.shape[1])


def solution(mesh):
    return jax.shard_map(
        shards,
        mesh=mesh,
        in_specs=(P(None, None, "freq", "chan"), P()),
        out_specs=P("chan", "freq", None),
        check_vma=False,
    )
```

time: 875 us -> 28.7 us (0.03)
  waiting for transfers between devices: 647 us -> 0 us
  local copies, waits for them, and re-layouts: 115 us -> 1.38 us
  other arithmetic: 46 us -> 0 us
  matrix products: 31.8 us -> 0 us
  Pallas kernels: 0 us -> 27.1 us
  between operations: 17.2 us -> 0.01 us
    reduce_scatter x1 -> x0, waiting for transfers between devices: 647 us -> none  [shards(): lax.psum_scatter(image_term, ('chan', 'freq'), scatter_dimension=0, tiled...]
    reshape x80 -> x0, local copies, waits for them, and re-layouts: 46.4 us -> none  [lag_sums(): skewed = padded.reshape(leading + (extent, extent + 1))]
    dot_general x48 -> x0, matrix products: 31.8 us -> none  [the longest x4 13.9 us: slant_terms(): jnp.einsum('gas,gt->ast', spectrum, kernel, precision=lax.Precision.HIGHEST)]
    pad x40 -> x0, local copies, waits for them, and re-layouts: 31.1 us -> none  [lag_sums(): padded = jnp.pad(flat_panel, [(0, 0)] * len(leading) + [(0, extent)])]
    pallas_call x0 -> x1, Pallas kernels: none -> 27.1 us  [shards(): pl.pallas_call(kernel, out_shape=jax.ShapeDtypeStruct((SLOWNESS // FREQ,...]
    while x184 -> x0, local copies, waits for them, and re-layouts: 24.3 us -> none
    sin x4 -> x0, other arithmetic: 16.7 us -> none  [slant_terms(): sine_part = jnp.sin(lag_angle)]
  transfers between devices with their start and end apart: 5 -> 0, of which waited for: 1 -> 0; matrix products, arithmetic and copies ran while one was open for 12% -> 0% of each run, Pallas kernels for 0% -> 0%
where the time goes in v1:
time: 28.7 us; the launch traced here: 28.5 us
  Pallas kernels  27.1 us (94%)
  local copies, waits for them, and re-layouts  1.38 us (5%)
    pallas_call x1, Pallas kernels, shards(): pl.pallas_call(kernel, out_shape=jax.ShapeDtypeStruct((SLOWNESS // FREQ,...  27.1 us
    unnamed x1, local copies, waits for them, and re-layouts  1.38 us

profile of v1, /device:TPU:1, one launch (start us, length us, event | category | flops | bytes accessed | tf_op | source)
XLA Modules:
  0.0 28.5 jit_solution(17994251077533830436)
XLA Ops:
  0.0 27.1 %slant_stack.1 = f32[16,512]{1,0:T(8,128)} custom-call(s32[8]{0:T(128)} %position_ref.1, bf16[64,8,2,128]{3,2,1,0:T(2,128)(2,1)} %bitcast.2), custom_call_target="tpu_custom_call" | custom-call | tf_op jit(solution)/shard_map/slant_stack/pallas_call | solution.py:273
  27.1 1.4 %copy.4 = f32[1,16,512]{2,1,0:T(8,128)} copy(f32[1,16,512]{2,1,0:T(8,128)} %bitcast.3) | data formatting | bytes 65536

commit v2 on v1

--- a/solution.py
+++ b/solution.py
@@ -58,6 +58,7 @@
     position_ref,
     spectra_ref,
     out_ref,
+    places,
     blocks,
     left,
     right,
@@ -67,19 +68,17 @@
     lag_low,
     time_high,
     time_low,
+    turned,
     terms,
-    gathered,
-    relayed,
     received,
-    turned,
     flipped,
+    ready,
+    place_sem,
     own_sem,
-    send_first,
-    recv_first,
-    send_second,
-    recv_second,
-    send_third,
-    recv_third,
+    send_block,
+    recv_block,
+    send_term,
+    recv_term,
 ):
     chan = lax.axis_index("chan")
     freq = lax.axis_index("freq")
@@ -101,21 +100,23 @@
         )
     own = pltpu.make_async_copy(spectra_ref.at[:, chan], blocks.at[chan], own_sem)
     own.start()
+    placing = pltpu.make_async_copy(position_ref, places, place_sem)
+    placing.start()
     pl.semaphore_wait(barrier, CHAN - 1 + FREQ - 1)
 
-    first = []
+    arrivals = []
     for step in range(1, CHAN):
         peer = lax.rem(chan + step, CHAN)
         copy = pltpu.make_async_remote_copy(
             src_ref=spectra_ref.at[:, peer],
             dst_ref=blocks.at[chan],
-            send_sem=send_first.at[step],
-            recv_sem=recv_first.at[step],
+            send_sem=send_block.at[step],
+            recv_sem=recv_block.at[step],
             device_id={"chan": peer},
             device_id_type=pl.DeviceIdType.MESH,
         )
         copy.start()
-        first.append(copy)
+        arrivals.append((step, copy))
 
     base_bin = 2 * CHAN * freq + 2 * chan
 
@@ -161,34 +162,52 @@
             time_high[at, :] = high
             time_low[at, :] = low
 
-    own.wait()
-    for copy in first:
-        copy.wait_recv()
-
     odd = iota((BLOCK, ROWS), 1) % 2
     mirror = iota((BLOCK, BLOCK), 0) + iota((BLOCK, BLOCK), 1) == BLOCK - 1
     mirror = jnp.where(mirror, 1.0, 0.0).astype(jnp.bfloat16)
+    half = ROWS // 2
+
+    def prepare(index):
+        value = blocks[index].reshape(ROWS, BLOCK)
+        right[index, :, pl.ds(0, BLOCK)] = value
+        right[index, pl.ds(0, half), pl.ds(BLOCK, BLOCK)] = value[half:]
+        right[index, pl.ds(half, half), pl.ds(BLOCK, BLOCK)] = -value[:half]
+        across = lax.dot_general(
+            mirror, value, (((1,), (1,)), ((), ())), preferred_element_type=jnp.float32
+        )
+        for bin_index in range(BINS):
+            left[index, pl.ds(bin_index * BLOCK, BLOCK), :] = jnp.where(
+                odd == bin_index, across, 0.0
+            ).astype(jnp.bfloat16)
+
+    own.wait()
+    prepare(chan)
+    for step, copy in arrivals:
+        copy.wait_recv()
+        prepare(lax.rem(chan - step + CHAN, CHAN))
+
+    for step in range(1, FREQ):
+        pl.semaphore_signal(
+            ready,
+            inc=1,
+            device_id={"freq": lax.rem(freq + step, FREQ)},
+            device_id_type=pl.DeviceIdType.MESH,
+        )
+
+    placing.wait()
+    at_place = []
     for place in range(CHAN):
         block = jnp.int32(0)
         for index in range(CHAN):
-            block = jnp.where(position_ref[index] == place, index, block)
-        value = blocks[block].reshape(ROWS, BLOCK)
-        half = ROWS // 2
-        right[pl.ds(place * ROWS, ROWS), pl.ds(0, BLOCK)] = value
-        right[pl.ds(place * ROWS, half), pl.ds(BLOCK, BLOCK)] = value[half:]
-        right[pl.ds(place * ROWS + half, half), pl.ds(BLOCK, BLOCK)] = -value[:half]
-        across = lax.dot_general(
-            mirror, value, (((1,), (1,)), ((), ())), preferred_element_type=jnp.float32
-        )
-        for bin_index in range(BINS):
-            left[pl.ds(bin_index * BLOCK, BLOCK), pl.ds(place * ROWS, ROWS)] = jnp.where(
-                odd == bin_index, across, 0.0
-            ).astype(jnp.bfloat16)
+            block = jnp.where(places[index] == place, index, block)
+        at_place.append(block)
 
     wrapped = iota((BLOCK, BLOCK), 0) > iota((BLOCK, BLOCK), 1)
     for delta in range(CHAN):
-        depth = (CHAN - delta) * ROWS
-        panels = dot(left[:, :depth], right[delta * ROWS :, :])
+        panels = dot(
+            jnp.concatenate([left[at_place[place]] for place in range(CHAN - delta)], axis=1),
+            jnp.concatenate([right[at_place[place]] for place in range(delta, CHAN)], axis=0),
+        )
         sums = []
         for bin_index in range(BINS):
             for part in range(2):
@@ -214,44 +233,29 @@
     row = iota((CHAN * SLABS, BLOCK), 0)
     lane = iota((CHAN * SLABS, BLOCK), 1)
     steps = (base_bin + lane // (2 * WIDE)) * (lane % WIDE) * (BLOCK * (row // SLABS))
-    terms[...] = slants[:, :BLOCK] * cosine(steps) + slants[:, BLOCK:] * cosine(steps - QUARTER)
-
-    second = []
-    for step in range(1, CHAN):
-        peer = lax.rem(chan + step, CHAN)
-        copy = pltpu.make_async_remote_copy(
-            src_ref=terms.at[pl.ds(pl.multiple_of(peer * SLABS, SLABS), SLABS), :],
-            dst_ref=gathered.at[chan],
-            send_sem=send_second.at[step],
-            recv_sem=recv_second.at[step],
-            device_id={"chan": peer},
-            device_id_type=pl.DeviceIdType.MESH,
-        )
-        copy.start()
-        second.append(copy)
-    gathered[chan] = terms[pl.ds(pl.multiple_of(chan * SLABS, SLABS), SLABS), :]
-    for copy in second:
-        copy.wait_recv()
-
-    for slab in range(SLABS):
-        relayed[slab] = gathered[:, slab, :]
-
-    third = []
-    for step in range(1, FREQ):
-        peer = lax.rem(freq + step, FREQ)
-        copy = pltpu.make_async_remote_copy(
-            src_ref=relayed.at[peer // 2],
-            dst_ref=received.at[freq],
-            send_sem=send_third.at[step],
-            recv_sem=recv_third.at[step],
-            device_id={"freq": peer},
-            device_id_type=pl.DeviceIdType.MESH,
-        )
-        copy.start()
-        third.append(copy)
-    received[freq] = relayed[freq // 2]
-    for copy in third:
-        copy.wait_recv()
+    slants = slants[:, :BLOCK] * cosine(steps) + slants[:, BLOCK:] * cosine(steps - QUARTER)
+    terms[...] = slants.reshape(CHAN * SLABS, 1, BLOCK)
+
+    pl.semaphore_wait(ready, FREQ - 1)
+    source = freq * CHAN + chan
+
+    def send(step, carry):
+        target = lax.rem(chan * FREQ + freq + step, CHAN * FREQ)
+        pltpu.make_async_remote_copy(
+            src_ref=terms.at[lax.div(target, 2)],
+            dst_ref=received.at[source],
+            send_sem=send_term,
+            recv_sem=recv_term,
+            device_id={"chan": lax.div(target, FREQ), "freq": lax.rem(target, FREQ)},
+            device_id_type=pl.DeviceIdType.MESH,
+        ).start()
+        return carry
+
+    others = CHAN * FREQ - 1
+    lax.fori_loop(1, others + 1, send, 0, unroll=8)
+    received[source] = terms[lax.div(chan * FREQ + freq, 2)]
+    everything = received.at[pl.ds(0, others)]
+    pltpu.make_async_copy(everything, everything, recv_term).wait()
 
     flipped[...] = received[...].reshape(FREQ * CHAN, BLOCK).T
     half_wide = WIDE // 2
@@ -263,8 +267,9 @@
     high, low = split(spectrum)
     out_ref[...] = dot(high, time_high[...]) + dot(low, time_high[...]) + dot(high, time_low[...])
 
-    for copy in first + second + third:
+    for step, copy in arrivals:
         copy.wait_send()
+    pltpu.make_async_copy(everything, everything, send_term).wait()
 
 
 def shards(spectra, block_position):
@@ -272,35 +277,34 @@
     view = spectra.reshape(2 * SEGMENTS, pairs, BINS, BLOCK)
     image = pl.pallas_call(
         kernel,
-        out_shape=jax.ShapeDtypeStruct((SLOWNESS // FREQ, LAG_TIMES), jnp.float32),
+        out_shape=pltpu.VMEM((SLOWNESS // FREQ, LAG_TIMES), jnp.float32),
         in_specs=[
-            pl.BlockSpec(memory_space=pltpu.SMEM),
+            pl.BlockSpec(memory_space=pl.ANY),
             pl.BlockSpec(memory_space=pl.ANY),
         ],
         out_specs=pl.BlockSpec(memory_space=pltpu.VMEM),
         scratch_shapes=[
+            pltpu.SMEM((CHAN,), jnp.int32),
             pltpu.VMEM((CHAN, 2 * SEGMENTS, BINS, BLOCK), jnp.bfloat16),
-            pltpu.VMEM((BINS * BLOCK, CHAN * ROWS), jnp.bfloat16),
-            pltpu.VMEM((CHAN * ROWS, 2 * BLOCK), jnp.bfloat16),
+            pltpu.VMEM((CHAN, BINS * BLOCK, ROWS), jnp.bfloat16),
+            pltpu.VMEM((CHAN, ROWS, 2 * BLOCK), jnp.bfloat16),
             pltpu.VMEM((BINS, CHAN * SLABS, 2 * BLOCK), jnp.float32),
             pltpu.VMEM((BINS, CHAN * SLABS, 2 * BLOCK), jnp.float32),
             pltpu.VMEM((BINS * 4 * BLOCK, 2 * BLOCK), jnp.bfloat16),
             pltpu.VMEM((BINS * 4 * BLOCK, 2 * BLOCK), jnp.bfloat16),
             pltpu.VMEM((2 * FREQS, LAG_TIMES), jnp.bfloat16),
             pltpu.VMEM((2 * FREQS, LAG_TIMES), jnp.bfloat16),
-            pltpu.VMEM((CHAN * SLABS, BLOCK), jnp.float32),
-            pltpu.VMEM((CHAN, SLABS, BLOCK), jnp.float32),
-            pltpu.VMEM((SLABS, CHAN, BLOCK), jnp.float32),
-            pltpu.VMEM((FREQ, CHAN, BLOCK), jnp.float32),
             pltpu.VMEM((CHAN * SLABS, BINS * 4 * BLOCK), jnp.float32),
+            pltpu.VMEM((CHAN * SLABS, 1, BLOCK), jnp.float32),
+            pltpu.VMEM((FREQ * CHAN, 1, BLOCK), jnp.float32),
             pltpu.VMEM((BLOCK, FREQ * CHAN), jnp.float32),
+            pltpu.SemaphoreType.REGULAR,
+            pltpu.SemaphoreType.DMA,
             pltpu.SemaphoreType.DMA,
             pltpu.SemaphoreType.DMA((CHAN,)),
             pltpu.SemaphoreType.DMA((CHAN,)),
-            pltpu.SemaphoreType.DMA((CHAN,)),
-            pltpu.SemaphoreType.DMA((CHAN,)),
-            pltpu.SemaphoreType.DMA((FREQ,)),
-            pltpu.SemaphoreType.DMA((FREQ,)),
+            pltpu.SemaphoreType.DMA,
+            pltpu.SemaphoreType.DMA,
         ],
         compiler_params=pltpu.CompilerParams(collective_id=0, has_side_effects=True),
         name="slant_stack",

time: 28.7 us -> 25.7 us (0.90)
  Pallas kernels: 27.1 us -> 25 us
  local copies, waits for them, and re-layouts: 1.38 us -> 0.62 us
    pallas_call x1, Pallas kernels: 27.1 us -> 25 us  [shards(): pl.pallas_call(kernel, out_shape=pltpu.VMEM((SLOWNESS // FREQ, LAG_TIMES)...]
    unnamed x1, local copies, waits for them, and re-layouts: 1.38 us -> 0.62 us
where the time goes in v2:
time: 25.7 us; the launch traced here: 25.6 us
  Pallas kernels  25 us (97%)
  local copies, waits for them, and re-layouts  0.62 us (2%)
    pallas_call x1, Pallas kernels, shards(): pl.pallas_call(kernel, out_shape=pltpu.VMEM((SLOWNESS // FREQ, LAG_TIMES)...  25 us
    unnamed x1, local copies, waits for them, and re-layouts  0.62 us

profile of v2, /device:TPU:1, one launch (start us, length us, event | category | flops | bytes accessed | tf_op | source)
XLA Modules:
  0.0 25.6 jit_solution(5577000226720757110)
XLA Ops:
  0.0 25.0 %slant_stack.1 = f32[16,512]{1,0:T(8,128)S(1)} custom-call(s32[8]{0:T(128)} %position_ref.1, bf16[64,8,2,128]{3,2,1,0:T(2,128)(2,1)} %bitcast.3), custom_call_target="tpu_custom_call" | custom-call | tf_op jit(solution)/shard_map/slant_stack/pallas_call | solution.py:278
  25.0 0.6 %copy.4 = f32[1,16,512]{2,1,0:T(8,128)} copy(f32[1,16,512]{2,1,0:T(8,128)S(1)} %bitcast.2) | data formatting | bytes 65536

commit v3 on v2

--- a/solution.py
+++ b/solution.py
@@ -1,4 +1,4 @@
-import functools
+import itertools
 import math
 
 import jax
@@ -18,9 +18,31 @@
 BINS = 2
 ROWS = 2 * SEGMENTS * BINS
 TURN = 8 * FREQS * BLOCK
+QUARTER = TURN // 4
 WIDE = 32
 SLABS = SLOWNESS // WIDE
+RING = 4
+OFFSETS = ((1, 0), (0, 1), (0, 3), (1, 1), (1, 3), (0, 2), (1, 2))
+SEND_ORDER = (0, 1, 2, 3, 4, 5, 6)
+WAIT_ORDER = (0, 1, 2, 3, 4, 5, 6)
 SINE = [(-1) ** k * (2 * math.pi) ** (2 * k + 1) / math.factorial(2 * k + 1) for k in range(7)]
+
+
+def hops(offset, chip):
+    along_y = (0, 1, 2, 1)[offset[0] + 2 * chip[0]]
+    return along_y + min(offset[1], RING - offset[1]) + min(chip[1], RING - chip[1])
+
+
+FAR_FIRST = sorted(
+    (
+        (offset, chip, turn)
+        for offset in itertools.product(range(2), range(RING))
+        for chip in itertools.product(range(2), range(RING))
+        for turn in range(2)
+        if (offset, chip, turn) != ((0, 0), (0, 0), 0)
+    ),
+    key=lambda other: -hops(other[0], other[1]),
+)
 
 
 def iota(shape, axis):
@@ -35,9 +57,6 @@
     for coefficient in SINE[-2::-1]:
         value = value * square + coefficient
     return value * turn
-
-
-QUARTER = TURN // 4
 
 
 def lag_at(place):
@@ -72,7 +91,8 @@
     terms,
     received,
     flipped,
-    ready,
+    told_nearby,
+    told_along,
     place_sem,
     own_sem,
     send_block,
@@ -83,30 +103,42 @@
     chan = lax.axis_index("chan")
     freq = lax.axis_index("freq")
 
+    ring, spot = lax.div(chan, RING), lax.rem(chan, RING)
+
+    def at_offset(offset):
+        return RING * lax.rem(ring + offset[0], 2) + lax.rem(spot + offset[1], RING)
+
+    def signal(semaphore, **target):
+        pl.semaphore_signal(
+            semaphore, inc=1, device_id=target, device_id_type=pl.DeviceIdType.MESH
+        )
+
+    core, over, across = lax.rem(freq, 2), lax.rem(lax.div(freq, 2), RING), lax.div(freq, 8)
+    facing = at_offset((1, 0))
+    opposite = lax.rem(freq + FREQ // 2, FREQ)
+    nearby = (
+        {"freq": freq + 1 - 2 * core},
+        {"chan": facing, "freq": opposite},
+        {"chan": facing, "freq": opposite + 1 - 2 * core},
+    )
+    along = tuple(
+        {"freq": 8 * across + 2 * lax.rem(over + step, RING) + core} for step in (2, 1, 3)
+    )
+
     barrier = pltpu.get_barrier_semaphore()
-    for step in range(1, CHAN):
-        pl.semaphore_signal(
-            barrier,
-            inc=1,
-            device_id={"chan": lax.rem(chan + step, CHAN)},
-            device_id_type=pl.DeviceIdType.MESH,
-        )
-    for step in range(1, FREQ):
-        pl.semaphore_signal(
-            barrier,
-            inc=1,
-            device_id={"freq": lax.rem(freq + step, FREQ)},
-            device_id_type=pl.DeviceIdType.MESH,
-        )
+    for offset in OFFSETS[::-1]:
+        signal(barrier, chan=at_offset(offset))
+    for other in along + nearby:
+        signal(barrier, **other)
     own = pltpu.make_async_copy(spectra_ref.at[:, chan], blocks.at[chan], own_sem)
     own.start()
     placing = pltpu.make_async_copy(position_ref, places, place_sem)
     placing.start()
-    pl.semaphore_wait(barrier, CHAN - 1 + FREQ - 1)
+    pl.semaphore_wait(barrier, len(OFFSETS) + 6)
 
     arrivals = []
-    for step in range(1, CHAN):
-        peer = lax.rem(chan + step, CHAN)
+    for step in SEND_ORDER:
+        peer = at_offset(OFFSETS[step])
         copy = pltpu.make_async_remote_copy(
             src_ref=spectra_ref.at[:, peer],
             dst_ref=blocks.at[chan],
@@ -117,6 +149,10 @@
         )
         copy.start()
         arrivals.append((step, copy))
+    arrivals.sort(key=lambda arrival: WAIT_ORDER.index(arrival[0]))
+
+    for other in nearby:
+        signal(told_nearby, **other)
 
     base_bin = 2 * CHAN * freq + 2 * chan
 
@@ -151,6 +187,10 @@
             lag_high[at, :] = high
             lag_low[at, :] = low
 
+    pl.semaphore_wait(told_nearby, 3)
+    for other in along:
+        signal(told_along, **other)
+
     scale = math.sqrt(SEGMENTS / FREQS)
     for bin_index in range(BINS):
         for part in range(2):
@@ -184,15 +224,7 @@
     prepare(chan)
     for step, copy in arrivals:
         copy.wait_recv()
-        prepare(lax.rem(chan - step + CHAN, CHAN))
-
-    for step in range(1, FREQ):
-        pl.semaphore_signal(
-            ready,
-            inc=1,
-            device_id={"freq": lax.rem(freq + step, FREQ)},
-            device_id_type=pl.DeviceIdType.MESH,
-        )
+        prepare(at_offset((OFFSETS[step][0], RING - OFFSETS[step][1])))
 
     placing.wait()
     at_place = []
@@ -236,23 +268,30 @@
     slants = slants[:, :BLOCK] * cosine(steps) + slants[:, BLOCK:] * cosine(steps - QUARTER)
     terms[...] = slants.reshape(CHAN * SLABS, 1, BLOCK)
 
-    pl.semaphore_wait(ready, FREQ - 1)
+    pl.semaphore_wait(told_along, 3)
     source = freq * CHAN + chan
-
-    def send(step, carry):
-        target = lax.rem(chan * FREQ + freq + step, CHAN * FREQ)
+    to_chan = {offset: at_offset(offset) for offset in OFFSETS + ((0, 0),)}
+    to_chip = {
+        (flip, step): RING * lax.rem(across + flip, 2) + lax.rem(over + step, RING)
+        for flip in range(2)
+        for step in range(RING)
+    }
+    to_freq = {
+        chip + (turn,): 2 * place + lax.rem(core + turn, 2)
+        for chip, place in to_chip.items()
+        for turn in range(2)
+    }
+    for offset, chip, turn in FAR_FIRST:
         pltpu.make_async_remote_copy(
-            src_ref=terms.at[lax.div(target, 2)],
+            src_ref=terms.at[to_chan[offset] * SLABS + to_chip[chip]],
             dst_ref=received.at[source],
             send_sem=send_term,
             recv_sem=recv_term,
-            device_id={"chan": lax.div(target, FREQ), "freq": lax.rem(target, FREQ)},
+            device_id={"chan": to_chan[offset], "freq": to_freq[chip + (turn,)]},
             device_id_type=pl.DeviceIdType.MESH,
         ).start()
-        return carry
 
     others = CHAN * FREQ - 1
-    lax.fori_loop(1, others + 1, send, 0, unroll=8)
     received[source] = terms[lax.div(chan * FREQ + freq, 2)]
     everything = received.at[pl.ds(0, others)]
     pltpu.make_async_copy(everything, everything, recv_term).wait()
@@ -299,6 +338,7 @@
             pltpu.VMEM((FREQ * CHAN, 1, BLOCK), jnp.float32),
             pltpu.VMEM((BLOCK, FREQ * CHAN), jnp.float32),
             pltpu.SemaphoreType.REGULAR,
+            pltpu.SemaphoreType.REGULAR,
             pltpu.SemaphoreType.DMA,
             pltpu.SemaphoreType.DMA,
             pltpu.SemaphoreType.DMA((CHAN,)),

time: 25.7 us -> 22.6 us (0.88)
  Pallas kernels: 25 us -> 21.9 us
    pallas_call x1, Pallas kernels: 25 us -> 21.9 us  [shards(): pl.pallas_call(kernel, out_shape=pltpu.VMEM((SLOWNESS // FREQ, LAG_TIMES)...]
where the time goes in v3:
time: 22.6 us; the launch traced here: 22.5 us
  Pallas kernels  21.9 us (97%)
  local copies, waits for them, and re-layouts  0.62 us (3%)
    pallas_call x1, Pallas kernels, shards(): pl.pallas_call(kernel, out_shape=pltpu.VMEM((SLOWNESS // FREQ, LAG_TIMES)...  21.9 us
    unnamed x1, local copies, waits for them, and re-layouts  0.62 us

profile of v3, /device:TPU:1, one launch (start us, length us, event | category | flops | bytes accessed | tf_op | source)
XLA Modules:
  0.0 22.5 jit_solution(13648462687441420462)
XLA Ops:
  0.0 21.9 %slant_stack.1 = f32[16,512]{1,0:T(8,128)S(1)} custom-call(s32[8]{0:T(128)} %position_ref.1, bf16[64,8,2,128]{3,2,1,0:T(2,128)(2,1)} %bitcast.3), custom_call_target="tpu_custom_call" | custom-call | tf_op jit(solution)/shard_map/slant_stack/pallas_call | solution.py:317
  21.9 0.6 %copy.4 = f32[1,16,512]{2,1,0:T(8,128)} copy(f32[1,16,512]{2,1,0:T(8,128)S(1)} %bitcast.2) | data formatting | bytes 65536

commit v4 on v3

--- a/solution.py
+++ b/solution.py
@@ -23,8 +23,7 @@
 SLABS = SLOWNESS // WIDE
 RING = 4
 OFFSETS = ((1, 0), (0, 1), (0, 3), (1, 1), (1, 3), (0, 2), (1, 2))
-SEND_ORDER = (0, 1, 2, 3, 4, 5, 6)
-WAIT_ORDER = (0, 1, 2, 3, 4, 5, 6)
+WAITS = ((0, 1), (2, 3), (4, 5), (6,))
 SINE = [(-1) ** k * (2 * math.pi) ** (2 * k + 1) / math.factorial(2 * k + 1) for k in range(7)]
 
 
@@ -73,11 +72,19 @@
     return jnp.dot(left, right, preferred_element_type=jnp.float32)
 
 
+def product(left, high, low):
+    rows = left.shape[0]
+    left_high, left_low = split(left)
+    both = dot(jnp.concatenate([left_high, left_low], axis=0), high)
+    return both[:rows] + both[rows:] + dot(left_high, low)
+
+
 def kernel(
     position_ref,
     spectra_ref,
     out_ref,
     places,
+    staged,
     blocks,
     left,
     right,
@@ -94,7 +101,7 @@
     told_nearby,
     told_along,
     place_sem,
-    own_sem,
+    stage_sem,
     send_block,
     recv_block,
     send_term,
@@ -130,17 +137,23 @@
         signal(barrier, chan=at_offset(offset))
     for other in along + nearby:
         signal(barrier, **other)
-    own = pltpu.make_async_copy(spectra_ref.at[:, chan], blocks.at[chan], own_sem)
-    own.start()
+    staging = [
+        pltpu.make_async_copy(spectra_ref.at[:, index], staged.at[index], stage_sem.at[index])
+        for index in range(CHAN)
+    ]
+    for copy in staging:
+        copy.start()
     placing = pltpu.make_async_copy(position_ref, places, place_sem)
     placing.start()
     pl.semaphore_wait(barrier, len(OFFSETS) + 6)
 
+    for copy in staging:
+        copy.wait()
     arrivals = []
-    for step in SEND_ORDER:
-        peer = at_offset(OFFSETS[step])
+    for offset in OFFSETS:
+        step, peer = len(arrivals), at_offset(offset)
         copy = pltpu.make_async_remote_copy(
-            src_ref=spectra_ref.at[:, peer],
+            src_ref=staged.at[peer],
             dst_ref=blocks.at[chan],
             send_sem=send_block.at[step],
             recv_sem=recv_block.at[step],
@@ -148,8 +161,7 @@
             device_id_type=pl.DeviceIdType.MESH,
         )
         copy.start()
-        arrivals.append((step, copy))
-    arrivals.sort(key=lambda arrival: WAIT_ORDER.index(arrival[0]))
+        arrivals.append(copy)
 
     for other in nearby:
         signal(told_nearby, **other)
@@ -169,23 +181,19 @@
         weight_cos[bin_index] = cosine(steps) * inverse
         weight_sin[bin_index] = cosine(steps - QUARTER) * inverse
 
+    row = iota((2 * BLOCK, BLOCK), 0)
+    lane = iota((2 * BLOCK, BLOCK), 1)
+    slow = lane % WIDE
+    part = (lane // WIDE) % 2
     for bin_index in range(BINS):
-        row = iota((2 * BLOCK, 2 * BLOCK), 0)
-        lane = iota((2 * BLOCK, 2 * BLOCK), 1)
-        lag = lag_at(row)
-        slow = lane % WIDE
-        part = (lane // WIDE) % 2
-        lane_bin = (lane // (2 * WIDE)) % BINS
-        swapped = lane // (2 * BINS * WIDE)
-        steps = (base_bin + bin_index) * slow * lag
-        quarter = jnp.where(swapped == 0, -part, 1 - part)
+        swapped = (lane < BLOCK // 2) == (bin_index == 1)
+        quarter = jnp.where(swapped, 1 - part, -part)
+        steps = (base_bin + bin_index) * slow * lag_at(row) + QUARTER * quarter
         for row_part in range(2):
-            turned_steps = steps + QUARTER * (quarter + row_part)
-            table = jnp.where(lane_bin == bin_index, cosine(turned_steps), 0.0)
-            high, low = split(table)
-            at = pl.ds((2 * bin_index + row_part) * 2 * BLOCK, 2 * BLOCK)
-            lag_high[at, :] = high
-            lag_low[at, :] = low
+            high, low = split(cosine(steps + QUARTER * row_part))
+            at = pl.ds(row_part * 2 * BLOCK, 2 * BLOCK)
+            lag_high[bin_index, at, :] = high
+            lag_low[bin_index, at, :] = low
 
     pl.semaphore_wait(told_nearby, 3)
     for other in along:
@@ -207,8 +215,8 @@
     mirror = jnp.where(mirror, 1.0, 0.0).astype(jnp.bfloat16)
     half = ROWS // 2
 
-    def prepare(index):
-        value = blocks[index].reshape(ROWS, BLOCK)
+    def prepare(index, source):
+        value = source[index].reshape(ROWS, BLOCK)
         right[index, :, pl.ds(0, BLOCK)] = value
         right[index, pl.ds(0, half), pl.ds(BLOCK, BLOCK)] = value[half:]
         right[index, pl.ds(half, half), pl.ds(BLOCK, BLOCK)] = -value[:half]
@@ -220,11 +228,13 @@
                 odd == bin_index, across, 0.0
             ).astype(jnp.bfloat16)
 
-    own.wait()
-    prepare(chan)
-    for step, copy in arrivals:
-        copy.wait_recv()
-        prepare(at_offset((OFFSETS[step][0], RING - OFFSETS[step][1])))
+    prepare(chan, staged)
+    for steps in WAITS:
+        for step in steps:
+            arrivals[step].wait_recv()
+        for step in steps:
+            along_y, along_z = OFFSETS[step]
+            prepare(at_offset((along_y, RING - along_z)), blocks)
 
     placing.wait()
     at_place = []
@@ -260,12 +270,17 @@
             pieces.append(real * by_sin + imag * by_cos)
         turned[at, :] = jnp.concatenate(pieces, axis=1)
 
-    high, low = split(turned[...])
-    slants = dot(high, lag_high[...]) + dot(low, lag_high[...]) + dot(high, lag_low[...])
+    by_bin = []
+    for bin_index in range(BINS):
+        value = turned[:, pl.ds(bin_index * 4 * BLOCK, 4 * BLOCK)]
+        by_bin.append(product(value, lag_high[bin_index], lag_low[bin_index]))
     row = iota((CHAN * SLABS, BLOCK), 0)
     lane = iota((CHAN * SLABS, BLOCK), 1)
+    first = lane < BLOCK // 2
+    plain = jnp.where(first, by_bin[0], by_bin[1])
+    swapped = pltpu.roll(jnp.where(first, by_bin[1], by_bin[0]), BLOCK // 2, 1)
     steps = (base_bin + lane // (2 * WIDE)) * (lane % WIDE) * (BLOCK * (row // SLABS))
-    slants = slants[:, :BLOCK] * cosine(steps) + slants[:, BLOCK:] * cosine(steps - QUARTER)
+    slants = plain * cosine(steps) + swapped * cosine(steps - QUARTER)
     terms[...] = slants.reshape(CHAN * SLABS, 1, BLOCK)
 
     pl.semaphore_wait(told_along, 3)
@@ -303,10 +318,9 @@
         [flipped[pl.ds(start + WIDE * index, half_wide), :] for index in range(2 * BINS)],
         axis=1,
     )
-    high, low = split(spectrum)
-    out_ref[...] = dot(high, time_high[...]) + dot(low, time_high[...]) + dot(high, time_low[...])
-
-    for step, copy in arrivals:
+    out_ref[...] = product(spectrum, time_high[...], time_low[...])
+
+    for copy in arrivals:
         copy.wait_send()
     pltpu.make_async_copy(everything, everything, send_term).wait()
 
@@ -325,12 +339,13 @@
         scratch_shapes=[
             pltpu.SMEM((CHAN,), jnp.int32),
             pltpu.VMEM((CHAN, 2 * SEGMENTS, BINS, BLOCK), jnp.bfloat16),
+            pltpu.VMEM((CHAN, 2 * SEGMENTS, BINS, BLOCK), jnp.bfloat16),
             pltpu.VMEM((CHAN, BINS * BLOCK, ROWS), jnp.bfloat16),
             pltpu.VMEM((CHAN, ROWS, 2 * BLOCK), jnp.bfloat16),
             pltpu.VMEM((BINS, CHAN * SLABS, 2 * BLOCK), jnp.float32),
             pltpu.VMEM((BINS, CHAN * SLABS, 2 * BLOCK), jnp.float32),
-            pltpu.VMEM((BINS * 4 * BLOCK, 2 * BLOCK), jnp.bfloat16),
-            pltpu.VMEM((BINS * 4 * BLOCK, 2 * BLOCK), jnp.bfloat16),
+            pltpu.VMEM((BINS, 4 * BLOCK, BLOCK), jnp.bfloat16),
+            pltpu.VMEM((BINS, 4 * BLOCK, BLOCK), jnp.bfloat16),
             pltpu.VMEM((2 * FREQS, LAG_TIMES), jnp.bfloat16),
             pltpu.VMEM((2 * FREQS, LAG_TIMES), jnp.bfloat16),
             pltpu.VMEM((CHAN * SLABS, BINS * 4 * BLOCK), jnp.float32),
@@ -340,7 +355,7 @@
             pltpu.SemaphoreType.REGULAR,
             pltpu.SemaphoreType.REGULAR,
             pltpu.SemaphoreType.DMA,
-            pltpu.SemaphoreType.DMA,
+            pltpu.SemaphoreType.DMA((CHAN,)),
             pltpu.SemaphoreType.DMA((CHAN,)),
             pltpu.SemaphoreType.DMA((CHAN,)),
             pltpu.SemaphoreType.DMA,

time: 22.6 us -> 22.1 us (0.978)
  Pallas kernels: 21.9 us -> 21.3 us
    pallas_call x1, Pallas kernels: 21.9 us -> 21.3 us  [shards(): pl.pallas_call(kernel, out_shape=pltpu.VMEM((SLOWNESS // FREQ, LAG_TIMES)...]
where the time goes in v4:
time: 22.1 us; the launch traced here: 22 us
  Pallas kernels  21.3 us (96%)
  local copies, waits for them, and re-layouts  0.62 us (3%)
    pallas_call x1, Pallas kernels, shards(): pl.pallas_call(kernel, out_shape=pltpu.VMEM((SLOWNESS // FREQ, LAG_TIMES)...  21.3 us
    unnamed x1, local copies, waits for them, and re-layouts  0.62 us

profile of v4, /device:TPU:1, one launch (start us, length us, event | category | flops | bytes accessed | tf_op | source)
XLA Modules:
  0.0 22.0 jit_solution(7591261267676364278)
XLA Ops:
  0.0 21.3 %slant_stack.1 = f32[16,512]{1,0:T(8,128)S(1)} custom-call(s32[8]{0:T(128)} %position_ref.1, bf16[64,8,2,128]{3,2,1,0:T(2,128)(2,1)} %bitcast.3), custom_call_target="tpu_custom_call" | custom-call | tf_op jit(solution)/shard_map/slant_stack/pallas_call | solution.py:331
  21.3 0.6 %copy.4 = f32[1,16,512]{2,1,0:T(8,128)} copy(f32[1,16,512]{2,1,0:T(8,128)S(1)} %bitcast.2) | data formatting | bytes 65536

commit v5 on v4

--- a/solution.py
+++ b/solution.py
@@ -24,23 +24,18 @@
 RING = 4
 OFFSETS = ((1, 0), (0, 1), (0, 3), (1, 1), (1, 3), (0, 2), (1, 2))
 WAITS = ((0, 1), (2, 3), (4, 5), (6,))
+DELTAS = ((0,), (4, 5, 1, 6, 2, 7, 3))
 SINE = [(-1) ** k * (2 * math.pi) ** (2 * k + 1) / math.factorial(2 * k + 1) for k in range(7)]
-
-
-def hops(offset, chip):
-    along_y = (0, 1, 2, 1)[offset[0] + 2 * chip[0]]
-    return along_y + min(offset[1], RING - offset[1]) + min(chip[1], RING - chip[1])
 
 
 FAR_FIRST = sorted(
     (
-        (offset, chip, turn)
-        for offset in itertools.product(range(2), range(RING))
+        (chip, turn)
         for chip in itertools.product(range(2), range(RING))
         for turn in range(2)
-        if (offset, chip, turn) != ((0, 0), (0, 0), 0)
+        if (chip, turn) != ((0, 0), 0)
     ),
-    key=lambda other: -hops(other[0], other[1]),
+    key=lambda other: -other[0][0] - min(other[0][1], RING - other[0][1]),
 )
 
 
@@ -94,6 +89,8 @@
     lag_low,
     time_high,
     time_low,
+    offset_cos,
+    offset_sin,
     turned,
     terms,
     received,
@@ -181,6 +178,12 @@
         weight_cos[bin_index] = cosine(steps) * inverse
         weight_sin[bin_index] = cosine(steps - QUARTER) * inverse
 
+    row = iota((CHAN * SLABS, BLOCK), 0)
+    lane = iota((CHAN * SLABS, BLOCK), 1)
+    steps = (base_bin + lane // (2 * WIDE)) * (lane % WIDE) * (BLOCK * (row // SLABS))
+    offset_cos[...] = cosine(steps)
+    offset_sin[...] = cosine(steps - QUARTER)
+
     row = iota((2 * BLOCK, BLOCK), 0)
     lane = iota((2 * BLOCK, BLOCK), 1)
     slow = lane % WIDE
@@ -245,7 +248,8 @@
         at_place.append(block)
 
     wrapped = iota((BLOCK, BLOCK), 0) > iota((BLOCK, BLOCK), 1)
-    for delta in range(CHAN):
+
+    def lag_terms(delta):
         panels = dot(
             jnp.concatenate([left[at_place[place]] for place in range(CHAN - delta)], axis=1),
             jnp.concatenate([right[at_place[place]] for place in range(delta, CHAN)], axis=0),
@@ -261,31 +265,32 @@
                 behind = jnp.sum(jnp.where(wrapped, 0.0, skewed), axis=0, keepdims=True)
                 sums.append(jnp.concatenate([ahead, behind], axis=1))
         at = pl.ds(delta * SLABS, SLABS)
-        pieces = []
         for bin_index in range(BINS):
             real, imag = sums[2 * bin_index], sums[2 * bin_index + 1]
             by_cos = weight_cos[bin_index, at, :]
             by_sin = weight_sin[bin_index, at, :]
-            pieces.append(real * by_cos - imag * by_sin)
-            pieces.append(real * by_sin + imag * by_cos)
-        turned[at, :] = jnp.concatenate(pieces, axis=1)
-
-    by_bin = []
-    for bin_index in range(BINS):
-        value = turned[:, pl.ds(bin_index * 4 * BLOCK, 4 * BLOCK)]
-        by_bin.append(product(value, lag_high[bin_index], lag_low[bin_index]))
-    row = iota((CHAN * SLABS, BLOCK), 0)
-    lane = iota((CHAN * SLABS, BLOCK), 1)
-    first = lane < BLOCK // 2
-    plain = jnp.where(first, by_bin[0], by_bin[1])
-    swapped = pltpu.roll(jnp.where(first, by_bin[1], by_bin[0]), BLOCK // 2, 1)
-    steps = (base_bin + lane // (2 * WIDE)) * (lane % WIDE) * (BLOCK * (row // SLABS))
-    slants = plain * cosine(steps) + swapped * cosine(steps - QUARTER)
-    terms[...] = slants.reshape(CHAN * SLABS, 1, BLOCK)
-
-    pl.semaphore_wait(told_along, 3)
+            turned[bin_index, at, pl.ds(0, 2 * BLOCK)] = real * by_cos - imag * by_sin
+            turned[bin_index, at, pl.ds(2 * BLOCK, 2 * BLOCK)] = real * by_sin + imag * by_cos
+
+    def slant_terms(deltas):
+        rows = [pl.ds(delta * SLABS, SLABS) for delta in deltas]
+        by_bin = [
+            product(
+                jnp.concatenate([turned[bin_index, at, :] for at in rows], axis=0),
+                lag_high[bin_index],
+                lag_low[bin_index],
+            )
+            for bin_index in range(BINS)
+        ]
+        first = iota(by_bin[0].shape, 1) < BLOCK // 2
+        plain = jnp.where(first, by_bin[0], by_bin[1])
+        swapped = pltpu.roll(jnp.where(first, by_bin[1], by_bin[0]), BLOCK // 2, 1)
+        for index, at in enumerate(rows):
+            part = slice(index * SLABS, (index + 1) * SLABS)
+            slants = plain[part] * offset_cos[at, :] + swapped[part] * offset_sin[at, :]
+            terms[at] = slants.reshape(SLABS, 1, BLOCK)
+
     source = freq * CHAN + chan
-    to_chan = {offset: at_offset(offset) for offset in OFFSETS + ((0, 0),)}
     to_chip = {
         (flip, step): RING * lax.rem(across + flip, 2) + lax.rem(over + step, RING)
         for flip in range(2)
@@ -296,15 +301,33 @@
         for chip, place in to_chip.items()
         for turn in range(2)
     }
-    for offset, chip, turn in FAR_FIRST:
+
+    def post(delta, chip, turn):
         pltpu.make_async_remote_copy(
-            src_ref=terms.at[to_chan[offset] * SLABS + to_chip[chip]],
+            src_ref=terms.at[delta * SLABS + to_chip[chip]],
             dst_ref=received.at[source],
             send_sem=send_term,
             recv_sem=recv_term,
-            device_id={"chan": to_chan[offset], "freq": to_freq[chip + (turn,)]},
+            device_id={"chan": delta, "freq": to_freq[chip + (turn,)]},
             device_id_type=pl.DeviceIdType.MESH,
         ).start()
+
+    def post_all(delta):
+        for chip, turn in FAR_FIRST:
+            post(delta, chip, turn)
+
+        @pl.when(chan != delta)
+        def _():
+            post(delta, (0, 0), 0)
+
+    for deltas in DELTAS:
+        for delta in deltas:
+            lag_terms(delta)
+        slant_terms(deltas)
+        if deltas == DELTAS[0]:
+            pl.semaphore_wait(told_along, 3)
+        for delta in deltas:
+            post_all(delta)
 
     others = CHAN * FREQ - 1
     received[source] = terms[lax.div(chan * FREQ + freq, 2)]
@@ -348,7 +371,9 @@
             pltpu.VMEM((BINS, 4 * BLOCK, BLOCK), jnp.bfloat16),
             pltpu.VMEM((2 * FREQS, LAG_TIMES), jnp.bfloat16),
             pltpu.VMEM((2 * FREQS, LAG_TIMES), jnp.bfloat16),
-            pltpu.VMEM((CHAN * SLABS, BINS * 4 * BLOCK), jnp.float32),
+            pltpu.VMEM((CHAN * SLABS, BLOCK), jnp.float32),
+            pltpu.VMEM((CHAN * SLABS, BLOCK), jnp.float32),
+            pltpu.VMEM((BINS, CHAN * SLABS, 4 * BLOCK), jnp.float32),
             pltpu.VMEM((CHAN * SLABS, 1, BLOCK), jnp.float32),
             pltpu.VMEM((FREQ * CHAN, 1, BLOCK), jnp.float32),
             pltpu.VMEM((BLOCK, FREQ * CHAN), jnp.float32),

time: 22.1 us -> 21.5 us (0.973)
  Pallas kernels: 21.3 us -> 20.7 us
    pallas_call x1, Pallas kernels: 21.3 us -> 20.7 us  [shards(): pl.pallas_call(kernel, out_shape=pltpu.VMEM((SLOWNESS // FREQ, LAG_TIMES)...]
where the time goes in v5:
time: 21.5 us; the launch traced here: 21.4 us
  Pallas kernels  20.7 us (96%)
  local copies, waits for them, and re-layouts  0.62 us (3%)
    pallas_call x1, Pallas kernels, shards(): pl.pallas_call(kernel, out_shape=pltpu.VMEM((SLOWNESS // FREQ, LAG_TIMES)...  20.7 us
    unnamed x1, local copies, waits for them, and re-layouts  0.62 us

profile of v5, /device:TPU:1, one launch (start us, length us, event | category | flops | bytes accessed | tf_op | source)
XLA Modules:
  0.0 21.4 jit_solution(13375227360162423762)
XLA Ops:
  0.0 20.7 %slant_stack.1 = f32[16,512]{1,0:T(8,128)S(1)} custom-call(s32[8]{0:T(128)} %position_ref.1, bf16[64,8,2,128]{3,2,1,0:T(2,128)(2,1)} %bitcast.3), custom_call_target="tpu_custom_call" | custom-call | tf_op jit(solution)/shard_map/slant_stack/pallas_call | solution.py:354
  20.8 0.6 %copy.4 = f32[1,16,512]{2,1,0:T(8,128)} copy(f32[1,16,512]{2,1,0:T(8,128)S(1)} %bitcast.2) | data formatting | bytes 65536

commit v6 on v5

--- a/solution.py
+++ b/solution.py
@@ -24,6 +24,7 @@
 RING = 4
 OFFSETS = ((1, 0), (0, 1), (0, 3), (1, 1), (1, 3), (0, 2), (1, 2))
 WAITS = ((0, 1), (2, 3), (4, 5), (6,))
+ALL = True
 DELTAS = ((0,), (4, 5, 1, 6, 2, 7, 3))
 SINE = [(-1) ** k * (2 * math.pi) ** (2 * k + 1) / math.factorial(2 * k + 1) for k in range(7)]
 
@@ -91,6 +92,7 @@
     time_low,
     offset_cos,
     offset_sin,
+    square,
     turned,
     terms,
     received,
@@ -231,13 +233,28 @@
                 odd == bin_index, across, 0.0
             ).astype(jnp.bfloat16)
 
+    def paired(indices):
+        return dot(
+            jnp.concatenate([left[index] for index in indices], axis=1),
+            jnp.concatenate([right[index] for index in indices], axis=0),
+        )
+
     prepare(chan, staged)
+    waiting = [chan]
     for steps in WAITS:
         for step in steps:
             arrivals[step].wait_recv()
         for step in steps:
             along_y, along_z = OFFSETS[step]
-            prepare(at_offset((along_y, RING - along_z)), blocks)
+            index = at_offset((along_y, RING - along_z))
+            prepare(index, blocks)
+            waiting.append(index)
+        if steps == WAITS[1]:
+            square[...] = paired(waiting)
+            waiting = []
+        elif ALL and steps == WAITS[2]:
+            square[...] += paired(waiting)
+            waiting = []
 
     placing.wait()
     at_place = []
@@ -250,10 +267,13 @@
     wrapped = iota((BLOCK, BLOCK), 0) > iota((BLOCK, BLOCK), 1)
 
     def lag_terms(delta):
-        panels = dot(
-            jnp.concatenate([left[at_place[place]] for place in range(CHAN - delta)], axis=1),
-            jnp.concatenate([right[at_place[place]] for place in range(delta, CHAN)], axis=0),
-        )
+        if delta == 0:
+            panels = square[...] + paired(waiting)
+        else:
+            panels = dot(
+                jnp.concatenate([left[at_place[place]] for place in range(CHAN - delta)], axis=1),
+                jnp.concatenate([right[at_place[place]] for place in range(delta, CHAN)], axis=0),
+            )
         sums = []
         for bin_index in range(BINS):
             for part in range(2):
@@ -261,24 +281,31 @@
                     bin_index * BLOCK : (bin_index + 1) * BLOCK, part * BLOCK : (part + 1) * BLOCK
                 ]
                 skewed = pltpu.roll(panel, 0, 1, stride=1, stride_axis=0)
-                ahead = jnp.sum(jnp.where(wrapped, skewed, 0.0), axis=0, keepdims=True)
-                behind = jnp.sum(jnp.where(wrapped, 0.0, skewed), axis=0, keepdims=True)
-                sums.append(jnp.concatenate([ahead, behind], axis=1))
+                lags = [jnp.sum(jnp.where(wrapped, skewed, 0.0), axis=0, keepdims=True)]
+                if delta > 0:
+                    lags.append(jnp.sum(jnp.where(wrapped, 0.0, skewed), axis=0, keepdims=True))
+                sums.append(jnp.concatenate(lags, axis=1))
         at = pl.ds(delta * SLABS, SLABS)
         for bin_index in range(BINS):
             real, imag = sums[2 * bin_index], sums[2 * bin_index + 1]
-            by_cos = weight_cos[bin_index, at, :]
-            by_sin = weight_sin[bin_index, at, :]
-            turned[bin_index, at, pl.ds(0, 2 * BLOCK)] = real * by_cos - imag * by_sin
-            turned[bin_index, at, pl.ds(2 * BLOCK, 2 * BLOCK)] = real * by_sin + imag * by_cos
+            width = real.shape[1]
+            by_cos = weight_cos[bin_index, at, pl.ds(0, width)]
+            by_sin = weight_sin[bin_index, at, pl.ds(0, width)]
+            turned[bin_index, at, pl.ds(0, width)] = real * by_cos - imag * by_sin
+            turned[bin_index, at, pl.ds(2 * BLOCK, width)] = real * by_sin + imag * by_cos
 
     def slant_terms(deltas):
         rows = [pl.ds(delta * SLABS, SLABS) for delta in deltas]
+        width = BLOCK if deltas == (0,) else 2 * BLOCK
+        lags = (pl.ds(0, width), pl.ds(2 * BLOCK, width))
         by_bin = [
             product(
-                jnp.concatenate([turned[bin_index, at, :] for at in rows], axis=0),
-                lag_high[bin_index],
-                lag_low[bin_index],
+                jnp.concatenate(
+                    [jnp.concatenate([turned[bin_index, at, part] for at in rows], axis=0) for part in lags],
+                    axis=1,
+                ),
+                jnp.concatenate([lag_high[bin_index, part, :] for part in lags], axis=0),
+                jnp.concatenate([lag_low[bin_index, part, :] for part in lags], axis=0),
             )
             for bin_index in range(BINS)
         ]
@@ -373,6 +400,7 @@
             pltpu.VMEM((2 * FREQS, LAG_TIMES), jnp.bfloat16),
             pltpu.VMEM((CHAN * SLABS, BLOCK), jnp.float32),
             pltpu.VMEM((CHAN * SLABS, BLOCK), jnp.float32),
+            pltpu.VMEM((BINS * BLOCK, 2 * BLOCK), jnp.float32),
             pltpu.VMEM((BINS, CHAN * SLABS, 4 * BLOCK), jnp.float32),
             pltpu.VMEM((CHAN * SLABS, 1, BLOCK), jnp.float32),
             pltpu.VMEM((FREQ * CHAN, 1, BLOCK), jnp.float32),

time: 21.5 us -> 21.2 us (0.986)
  Pallas kernels: 20.7 us -> 20.4 us
    pallas_call x1, Pallas kernels: 20.7 us -> 20.4 us  [shards(): pl.pallas_call(kernel, out_shape=pltpu.VMEM((SLOWNESS // FREQ, LAG_TIMES)...]
where the time goes in v6:
time: 21.2 us; the launch traced here: 21.1 us
  Pallas kernels  20.4 us (96%)
  local copies, waits for them, and re-layouts  0.62 us (3%)
    pallas_call x1, Pallas kernels, shards(): pl.pallas_call(kernel, out_shape=pltpu.VMEM((SLOWNESS // FREQ, LAG_TIMES)...  20.4 us
    unnamed x1, local copies, waits for them, and re-layouts  0.62 us

profile of v6, /device:TPU:1, one launch (start us, length us, event | category | flops | bytes accessed | tf_op | source)
XLA Modules:
  0.0 21.1 jit_solution(17245067681774626617)
XLA Ops:
  0.0 20.4 %slant_stack.1 = f32[16,512]{1,0:T(8,128)S(1)} custom-call(s32[8]{0:T(128)} %position_ref.1, bf16[64,8,2,128]{3,2,1,0:T(2,128)(2,1)} %bitcast.3), custom_call_target="tpu_custom_call" | custom-call | tf_op jit(solution)/shard_map/slant_stack/pallas_call | solution.py:381
  20.4 0.6 %copy.4 = f32[1,16,512]{2,1,0:T(8,128)} copy(f32[1,16,512]{2,1,0:T(8,128)S(1)} %bitcast.2) | data formatting | bytes 65536

commit v7 on v6

--- a/solution.py
+++ b/solution.py
@@ -25,7 +25,7 @@
 OFFSETS = ((1, 0), (0, 1), (0, 3), (1, 1), (1, 3), (0, 2), (1, 2))
 WAITS = ((0, 1), (2, 3), (4, 5), (6,))
 ALL = True
-DELTAS = ((0,), (4, 5, 1, 6, 2, 7, 3))
+DELTAS = ((0,), (1, 4, 5), (2, 3, 6, 7))
 SINE = [(-1) ** k * (2 * math.pi) ** (2 * k + 1) / math.factorial(2 * k + 1) for k in range(7)]
 
 
@@ -109,26 +109,26 @@
     chan = lax.axis_index("chan")
     freq = lax.axis_index("freq")
 
-    ring, spot = lax.div(chan, RING), lax.rem(chan, RING)
+    ring, spot = chan >> 2, chan & 3
 
     def at_offset(offset):
-        return RING * lax.rem(ring + offset[0], 2) + lax.rem(spot + offset[1], RING)
+        return RING * ((ring + offset[0]) & 1) + ((spot + offset[1]) & 3)
 
     def signal(semaphore, **target):
         pl.semaphore_signal(
             semaphore, inc=1, device_id=target, device_id_type=pl.DeviceIdType.MESH
         )
 
-    core, over, across = lax.rem(freq, 2), lax.rem(lax.div(freq, 2), RING), lax.div(freq, 8)
+    core, over, across = freq & 1, (freq >> 1) & 3, freq >> 3
     facing = at_offset((1, 0))
-    opposite = lax.rem(freq + FREQ // 2, FREQ)
+    opposite = (freq + FREQ // 2) & (FREQ - 1)
     nearby = (
         {"freq": freq + 1 - 2 * core},
         {"chan": facing, "freq": opposite},
         {"chan": facing, "freq": opposite + 1 - 2 * core},
     )
     along = tuple(
-        {"freq": 8 * across + 2 * lax.rem(over + step, RING) + core} for step in (2, 1, 3)
+        {"freq": 8 * across + 2 * ((over + step) & 3) + core} for step in (2, 1, 3)
     )
 
     barrier = pltpu.get_barrier_semaphore()
@@ -215,6 +215,14 @@
             time_high[at, :] = high
             time_low[at, :] = low
 
+    placing.wait()
+    at_place = []
+    for place in range(CHAN):
+        block = jnp.int32(0)
+        for index in range(CHAN):
+            block = jnp.where(places[index] == place, index, block)
+        at_place.append(block)
+
     odd = iota((BLOCK, ROWS), 1) % 2
     mirror = iota((BLOCK, BLOCK), 0) + iota((BLOCK, BLOCK), 1) == BLOCK - 1
     mirror = jnp.where(mirror, 1.0, 0.0).astype(jnp.bfloat16)
@@ -242,6 +250,8 @@
     prepare(chan, staged)
     waiting = [chan]
     for steps in WAITS:
+        if steps == WAITS[-1]:
+            pl.semaphore_wait(told_along, 3)
         for step in steps:
             arrivals[step].wait_recv()
         for step in steps:
@@ -255,14 +265,6 @@
         elif ALL and steps == WAITS[2]:
             square[...] += paired(waiting)
             waiting = []
-
-    placing.wait()
-    at_place = []
-    for place in range(CHAN):
-        block = jnp.int32(0)
-        for index in range(CHAN):
-            block = jnp.where(places[index] == place, index, block)
-        at_place.append(block)
 
     wrapped = iota((BLOCK, BLOCK), 0) > iota((BLOCK, BLOCK), 1)
 
@@ -319,12 +321,12 @@
 
     source = freq * CHAN + chan
     to_chip = {
-        (flip, step): RING * lax.rem(across + flip, 2) + lax.rem(over + step, RING)
+        (flip, step): RING * ((across + flip) & 1) + ((over + step) & 3)
         for flip in range(2)
         for step in range(RING)
     }
     to_freq = {
-        chip + (turn,): 2 * place + lax.rem(core + turn, 2)
+        chip + (turn,): 2 * place + ((core + turn) & 1)
         for chip, place in to_chip.items()
         for turn in range(2)
     }
@@ -351,28 +353,25 @@
         for delta in deltas:
             lag_terms(delta)
         slant_terms(deltas)
-        if deltas == DELTAS[0]:
-            pl.semaphore_wait(told_along, 3)
         for delta in deltas:
             post_all(delta)
 
     others = CHAN * FREQ - 1
-    received[source] = terms[lax.div(chan * FREQ + freq, 2)]
+    received[source] = terms[(chan * FREQ + freq) >> 1]
     everything = received.at[pl.ds(0, others)]
+    for copy in arrivals:
+        copy.wait_send()
+    pltpu.make_async_copy(everything, everything, send_term).wait()
     pltpu.make_async_copy(everything, everything, recv_term).wait()
 
     flipped[...] = received[...].reshape(FREQ * CHAN, BLOCK).T
     half_wide = WIDE // 2
-    start = pl.multiple_of(lax.rem(freq, 2) * half_wide, half_wide)
+    start = pl.multiple_of(core * half_wide, half_wide)
     spectrum = jnp.concatenate(
         [flipped[pl.ds(start + WIDE * index, half_wide), :] for index in range(2 * BINS)],
         axis=1,
     )
     out_ref[...] = product(spectrum, time_high[...], time_low[...])
-
-    for copy in arrivals:
-        copy.wait_send()
-    pltpu.make_async_copy(everything, everything, send_term).wait()
 
 
 def shards(spectra, block_position):

time: 21.2 us -> 21.1 us (level)
  no operation moved by 1% of the time
where the time goes in v7:
time: 21.1 us; the launch traced here: 21 us
  Pallas kernels  20.4 us (97%)
  local copies, waits for them, and re-layouts  0.62 us (3%)
    pallas_call x1, Pallas kernels, shards(): pl.pallas_call(kernel, out_shape=pltpu.VMEM((SLOWNESS // FREQ, LAG_TIMES)...  20.4 us
    unnamed x1, local copies, waits for them, and re-layouts  0.62 us

profile of v7, /device:TPU:1, one launch (start us, length us, event | category | flops | bytes accessed | tf_op | source)
XLA Modules:
  0.0 21.0 jit_solution(7905633109396610587)
XLA Ops:
  0.0 20.4 %slant_stack.1 = f32[16,512]{1,0:T(8,128)S(1)} custom-call(s32[8]{0:T(128)} %position_ref.1, bf16[64,8,2,128]{3,2,1,0:T(2,128)(2,1)} %bitcast.3), custom_call_target="tpu_custom_call" | custom-call | tf_op jit(solution)/shard_map/slant_stack/pallas_call | solution.py:380
  20.4 0.6 %copy.4 = f32[1,16,512]{2,1,0:T(8,128)} copy(f32[1,16,512]{2,1,0:T(8,128)S(1)} %bitcast.2) | data formatting | bytes 65536

commit v8 on v7

--- a/solution.py
+++ b/solution.py
@@ -96,7 +96,6 @@
     turned,
     terms,
     received,
-    flipped,
     told_nearby,
     told_along,
     place_sem,
@@ -230,16 +229,17 @@
 
     def prepare(index, source):
         value = source[index].reshape(ROWS, BLOCK)
-        right[index, :, pl.ds(0, BLOCK)] = value
-        right[index, pl.ds(0, half), pl.ds(BLOCK, BLOCK)] = value[half:]
-        right[index, pl.ds(half, half), pl.ds(BLOCK, BLOCK)] = -value[:half]
+        swapped = jnp.concatenate([value[half:], -value[:half]], axis=0)
+        both = jnp.concatenate([value, swapped], axis=1)
         across = lax.dot_general(
             mirror, value, (((1,), (1,)), ((), ())), preferred_element_type=jnp.float32
         )
-        for bin_index in range(BINS):
-            left[index, pl.ds(bin_index * BLOCK, BLOCK), :] = jnp.where(
-                odd == bin_index, across, 0.0
-            ).astype(jnp.bfloat16)
+        masked = jnp.concatenate(
+            [jnp.where(odd == bin_index, across, 0.0) for bin_index in range(BINS)], axis=0
+        ).astype(jnp.bfloat16)
+        right[index] = both
+        left[index] = masked
+        return masked, both
 
     def paired(indices):
         return dot(
@@ -257,7 +257,7 @@
         for step in steps:
             along_y, along_z = OFFSETS[step]
             index = at_offset((along_y, RING - along_z))
-            prepare(index, blocks)
+            newest = prepare(index, blocks)
             waiting.append(index)
         if steps == WAITS[1]:
             square[...] = paired(waiting)
@@ -270,7 +270,7 @@
 
     def lag_terms(delta):
         if delta == 0:
-            panels = square[...] + paired(waiting)
+            panels = square[...] + dot(*newest)
         else:
             panels = dot(
                 jnp.concatenate([left[at_place[place]] for place in range(CHAN - delta)], axis=1),
@@ -364,13 +364,16 @@
     pltpu.make_async_copy(everything, everything, send_term).wait()
     pltpu.make_async_copy(everything, everything, recv_term).wait()
 
-    flipped[...] = received[...].reshape(FREQ * CHAN, BLOCK).T
+    flipped = received[...].reshape(FREQ * CHAN, BLOCK).T
     half_wide = WIDE // 2
-    start = pl.multiple_of(core * half_wide, half_wide)
-    spectrum = jnp.concatenate(
-        [flipped[pl.ds(start + WIDE * index, half_wide), :] for index in range(2 * BINS)],
-        axis=1,
-    )
+    halves = [
+        jnp.concatenate(
+            [flipped[start + WIDE * index : start + WIDE * index + half_wide] for index in range(2 * BINS)],
+            axis=1,
+        )
+        for start in (0, half_wide)
+    ]
+    spectrum = jnp.where(core == 0, halves[0], halves[1])
     out_ref[...] = product(spectrum, time_high[...], time_low[...])
 
 
@@ -403,7 +406,6 @@
             pltpu.VMEM((BINS, CHAN * SLABS, 4 * BLOCK), jnp.float32),
             pltpu.VMEM((CHAN * SLABS, 1, BLOCK), jnp.float32),
             pltpu.VMEM((FREQ * CHAN, 1, BLOCK), jnp.float32),
-            pltpu.VMEM((BLOCK, FREQ * CHAN), jnp.float32),
             pltpu.SemaphoreType.REGULAR,
             pltpu.SemaphoreType.REGULAR,
             pltpu.SemaphoreType.DMA,

time: 21.1 us -> 21.1 us (level)
  no operation moved by 1% of the time
where the time goes in v8:
time: 21.1 us; the launch traced here: 21 us
  Pallas kernels  20.4 us (97%)
  local copies, waits for them, and re-layouts  0.62 us (3%)
    pallas_call x1, Pallas kernels, shards(): pl.pallas_call(kernel, out_shape=pltpu.VMEM((SLOWNESS // FREQ, LAG_TIMES)...  20.4 us
    unnamed x1, local copies, waits for them, and re-layouts  0.62 us

profile of v8, /device:TPU:1, one launch (start us, length us, event | category | flops | bytes accessed | tf_op | source)
XLA Modules:
  0.0 21.0 jit_solution(15741517186008730047)
XLA Ops:
  0.0 20.4 %slant_stack.1 = f32[16,512]{1,0:T(8,128)S(1)} custom-call(s32[8]{0:T(128)} %position_ref.1, bf16[64,8,2,128]{3,2,1,0:T(2,128)(2,1)} %bitcast.3), custom_call_target="tpu_custom_call" | custom-call | tf_op jit(solution)/shard_map/slant_stack/pallas_call | solution.py:383
  20.4 0.6 %copy.4 = f32[1,16,512]{2,1,0:T(8,128)} copy(f32[1,16,512]{2,1,0:T(8,128)S(1)} %bitcast.2) | data formatting | bytes 65536

commit v9 on v8

--- a/solution.py
+++ b/solution.py
@@ -25,7 +25,7 @@
 OFFSETS = ((1, 0), (0, 1), (0, 3), (1, 1), (1, 3), (0, 2), (1, 2))
 WAITS = ((0, 1), (2, 3), (4, 5), (6,))
 ALL = True
-DELTAS = ((0,), (1, 4, 5), (2, 3, 6, 7))
+DELTAS = ((0,), (1, 4), (2, 3, 5, 6, 7))
 SINE = [(-1) ** k * (2 * math.pi) ** (2 * k + 1) / math.factorial(2 * k + 1) for k in range(7)]
 
 

time: 21.1 us -> 21.1 us (level)
  no operation moved by 1% of the time
where the time goes in v9:
time: 21.1 us; the launch traced here: 21 us
  Pallas kernels  20.4 us (97%)
  local copies, waits for them, and re-layouts  0.62 us (3%)
    pallas_call x1, Pallas kernels, shards(): pl.pallas_call(kernel, out_shape=pltpu.VMEM((SLOWNESS // FREQ, LAG_TIMES)...  20.4 us
    unnamed x1, local copies, waits for them, and re-layouts  0.62 us

profile of v9, /device:TPU:1, one launch (start us, length us, event | category | flops | bytes accessed | tf_op | source)
XLA Modules:
  0.0 21.0 jit_solution(12038288967570180833)
XLA Ops:
  0.0 20.4 %slant_stack.1 = f32[16,512]{1,0:T(8,128)S(1)} custom-call(s32[8]{0:T(128)} %position_ref.1, bf16[64,8,2,128]{3,2,1,0:T(2,128)(2,1)} %bitcast.3), custom_call_target="tpu_custom_call" | custom-call | tf_op jit(solution)/shard_map/slant_stack/pallas_call | solution.py:383
  20.4 0.6 %copy.4 = f32[1,16,512]{2,1,0:T(8,128)} copy(f32[1,16,512]{2,1,0:T(8,128)S(1)} %bitcast.2) | data formatting | bytes 65536
